TPU v7x, 32 devices: a whole 2x2x4 slice. The times are simulated.
32 devices in a mesh: row: 4 (over y, x), col: 8 (over z, core).
Axes of the slice: x: 2, y: 2, z: 4, core: 2. Of those that a mesh axis runs over, the one named last changes fastest.
Arguments:
- chol_factor: bfloat16 [32768, 32768], P('row', 'col')
- normals: bfloat16 [512, 32768], P('row', 'col'), may hold values from -6 to 6
- site_median: float32 [32768], P(('row', 'col')), may hold values from -3 to 3
- site_region: int32 [32768, 1], replicated, may hold values from 0 to 31; in each aligned block of 1024 rows (0 to 1023, 1024 to 2047, ...) at most 64 rows name the same one
- asset_pick: int32 [131072], P(('row', 'col')), may hold values from 0 to 65535
- asset_zone: int32 [131072], P(('row', 'col')), may hold values from 0 to 4095, as said below
- asset_capacity: float32 [131072], P(('row', 'col')), may hold values from -1.5 to 1.5
- asset_beta: float32 [131072], P(('row', 'col')), may hold values from 0.3 to 0.8
- asset_value: float32 [131072], P(('row', 'col')), may hold values from 0.005 to 0.05
Outputs:
- zone_loss: float32 [4096, 512], P(('row', 'col'))
Inputs may be any that keep to these rules, and one draw needn't show every extreme that they name: `site_region`: every region has at least one site; within each aligned block of 1024 sites no region has more than 64 sites, and some region has exactly 64. `asset_zone`: within each aligned block of 4096 assets, exactly 128 assets fall in each aligned run of 128 zones.
All inputs are finite; a program needn't handle non-finite values.
Results may differ from a plain program's by a relative error of at most 0.0012.
Values may be sent and summed in bfloat16 or wider, within the bound.
A program may use at most 128 MiB of HBM per device.

v0:
```python
import jax
import jax.numpy as jnp
from jax import lax
from jax.sharding import PartitionSpec as P

ZONES = 4096


def normal_cdf(argument):
    return 0.5 * (1.0 + jax.scipy.special.erf(argument * 0.7071067811865476))


def rank_within(onehot_table):
    running = jnp.cumsum(onehot_table, axis=0) - onehot_table
    return jnp.sum(running * onehot_table, axis=1)


def per_device(
    chol_factor,
    normals,
    site_median,
    site_region,
    asset_pick,
    asset_zone,
    asset_capacity,
    asset_beta,
    asset_value,
):
    panel_rows = lax.all_gather(normals, "row", axis=0, tiled=True)
    field_sum = lax.psum_scatter(
        lax.dot_general(
            chol_factor, panel_rows, (((1,), (1,)), ((), ())), preferred_element_type=jnp.float32
        ),
        "col",
        scatter_dimension=0,
        tiled=True,
    )
    log_motion = (site_median[:, None] + field_sum).astype(jnp.bfloat16)
    device_count = lax.axis_size("row") * lax.axis_size("col")
    own_index = lax.axis_index(("row", "col"))
    site_count = log_motion.shape[0]
    event_count = log_motion.shape[1]
    slot_cap = max(2, 2 * site_count // device_count)
    all_regions = site_region[:, 0].reshape(device_count, site_count)
    block_regions = lax.dynamic_index_in_dim(all_regions, own_index, 0, keepdims=False)
    region_table = (
        block_regions[:, None] == jnp.arange(device_count, dtype=jnp.int32)[None, :]
    ).astype(jnp.int32)
    position = block_regions * slot_cap + rank_within(region_table)
    selector = (
        position[None, :] == jnp.arange(device_count * slot_cap, dtype=jnp.int32)[:, None]
    ).astype(jnp.bfloat16)
    outgoing = jnp.dot(selector, log_motion, preferred_element_type=jnp.float32).astype(
        jnp.bfloat16
    )
    outgoing = outgoing.reshape(device_count, slot_cap, event_count)
    incoming = lax.all_to_all(
        outgoing, ("row", "col"), split_axis=0, concat_axis=0, tiled=True
    ).reshape(device_count * slot_cap, event_count)
    counts = jnp.sum((all_regions == own_index).astype(jnp.int32), axis=1)
    filled = (
        (jnp.arange(slot_cap, dtype=jnp.int32)[None, :] < counts[:, None])
        .astype(jnp.int32)
        .reshape(-1)
    )
    running = jnp.cumsum(filled)
    chosen = asset_pick % running[-1]
    slot_index = jnp.searchsorted(running, chosen + 1, side="left")
    motion = incoming[slot_index].astype(jnp.float32)
    damage = (
        asset_value[:, None] * normal_cdf((motion - asset_capacity[:, None]) / asset_beta[:, None])
    ).astype(jnp.bfloat16)
    zone_share = ZONES // device_count
    per_owner = asset_pick.shape[0] // device_count
    zone_owner = asset_zone // zone_share
    owner_table = (
        zone_owner[:, None] == jnp.arange(device_count, dtype=jnp.int32)[None, :]
    ).astype(jnp.int32)
    placing = zone_owner * per_owner + rank_within(owner_table)
    payload = (
        jnp.zeros_like(damage).at[placing].set(damage).reshape(device_count, per_owner, event_count)
    )
    inner_zone = asset_zone % zone_share
    local_labels = (
        jnp.zeros((damage.shape[0],), jnp.int32)
        .at[placing]
        .set(inner_zone)
        .reshape(device_count, per_owner)
    )
    member = (
        local_labels[:, :, None] == jnp.arange(zone_share, dtype=jnp.int32)[None, None, :]
    ).astype(jnp.bfloat16)
    zone_table = jnp.einsum("dpz,dpe->dze", member, payload, preferred_element_type=jnp.float32)
    zone_table = zone_table.reshape(device_count * zone_share, event_count)
    return lax.psum_scatter(zone_table, ("row", "col"), scatter_dimension=0, tiled=True)


def solution(mesh):
    in_specs = (
        P("row", "col"),
        P("row", "col"),
        P(("row", "col")),
        P(),
        P(("row", "col")),
        P(("row", "col")),
        P(("row", "col")),
        P(("row", "col")),
        P(("row", "col")),
    )
    out_specs = P(("row", "col"), None)
    return jax.shard_map(
        per_device, mesh=mesh, in_specs=in_specs, out_specs=out_specs, check_vma=False
    )
```

profile of v0, /device:TPU:0, one launch (start us, length us, event | category | flops | bytes accessed | tf_op | source)
XLA Modules:
  0.0 798.6 jit_solution(9510923057993495164)
XLA Ops:
  6.5 0.7 all-gather.2.cloned.1.call-update
  7.3 57.2 %all-gather.2.cloned.1.call-done = bf16[512,4096]{1,0:T(8,128)(2,1)} async-done(((bf16[128,4096]{1,0:T(8,128)(2,1)}), bf16[512,4096]{1,0:T(8,128)(2,1)}) %all-gather.2.cloned.1.call-update) | async-done | bytes 4194320 | tf_op jit(solution)/shard_map/all_gather | solution.py:29
  64.5 43.1 %fusion.28 = f32[8192,512]{1,0:T(8,128)} fusion(bf16[8192,4096]{1,0:T(8,128)(2,1)} %param.11, bf16[512,4096]{1,0:T(8,128)(2,1)} %all-gather.2.cloned.1.call-done), kind=kOutput, calls=%fused_computation.65 | convolution fusion | flops 34359738368 | bytes 88080384 | tf_op jit(solution)/shard_map/dot_general | solution.py:31
  107.7 0.5 broadcast.134
  108.2 0.3 copy-done
  108.5 0.9 reduce.7
  109.9 0.3 reduce-window.29
  110.5 0.6 slice.39
  112.4 9.0 %reduce-window.25 = s32[32,8,128]{2,1,0:T(8,128)S(1)} reduce-window(s32[32,8,128]{2,1,0:T(8,128)S(1)} %fusion.20, s32[]{:T(128)} %constant.89.clone.1), window={size=1x1x128 pad=0_0x0_0x127_0}, to_apply=%region_4.5 | reduce-window | flops 4161536 | bytes 262148 | tf_op jit(solution)/shard_map/reduce-window.2
  122.2 153.7 %reduce-scatter.3.cloned.1.call-done = f32[1024,512]{1,0:T(8,128)} async-done(((f32[8192,512]{1,0:T(8,128)}), f32[1024,512]{1,0:T(8,128)}) %reduce-scatter.3.cloned.1.call-update) | async-done | bytes 2097168 | tf_op jit(solution)/shard_map/reduce_scatter | solution.py:30
  275.9 5.4 fusion.8
  281.3 3.3 all-to-all-start
  284.8 277.5 %while.24 = (s32[]{:T(128)}, u32[4096]{0:T(1024)S(1)}, u32[4096]{0:T(1024)S(1)}, s32[2048]{0:T(1024)S(1)}, s32[4096]{0:T(1024)S(1)}, /*index=5*/s32[]{:T(128)}, s32[]{:T(128)}, s32[]{}) while((s32[]{:T(128)}, u32[4096]{0:T(1024)S(1)}, u32[4096]{0:T(1024)S(1)}, s32[2048]{0:T(1024)S(1)}, s32[4096]{0:T(1024)S(1)}, ...), condition=%wide.region_12.13_spmd.clone, body=%wide.region_11.12_spmd.clone.sunk | while | flops 77828 | bytes 270445 | solution.py:68
  284.8 23.0 %gather_fusion = s32[4096]{0:T(1024)S(1)} fusion(s32[2048]{0:T(1024)S(1)} %get-tuple-element.159, u32[4096]{0:T(1024)S(1)} %broadcast_clamp_fusion.2), kind=kCustom, calls=%fused_computation.clone.clone.1 | custom fusion | bytes 49152 | tf_op jit(solution)/shard_map/jit(searchsorted)/jit(_searchsorted_scan_impl)/vmap(jit(_searchsorted_scan_impl))/while/body/eval_jaxpr/gather | solution.py:68
  308.0 23.0 %gather_fusion = s32[4096]{0:T(1024)S(1)} fusion(s32[2048]{0:T(1024)S(1)} %get-tuple-element.159, u32[4096]{0:T(1024)S(1)} %broadcast_clamp_fusion.2), kind=kCustom, calls=%fused_computation.clone.clone.1 | custom fusion | bytes 49152 | tf_op jit(solution)/shard_map/jit(searchsorted)/jit(_searchsorted_scan_impl)/vmap(jit(_searchsorted_scan_impl))/while/body/eval_jaxpr/gather | solution.py:68
  331.1 23.0 %gather_fusion = s32[4096]{0:T(1024)S(1)} fusion(s32[2048]{0:T(1024)S(1)} %get-tuple-element.159, u32[4096]{0:T(1024)S(1)} %broadcast_clamp_fusion.2), kind=kCustom, calls=%fused_computation.clone.clone.1 | custom fusion | bytes 49152 | tf_op jit(solution)/shard_map/jit(searchsorted)/jit(_searchsorted_scan_impl)/vmap(jit(_searchsorted_scan_impl))/while/body/eval_jaxpr/gather | solution.py:68
  354.2 23.0 %gather_fusion = s32[4096]{0:T(1024)S(1)} fusion(s32[2048]{0:T(1024)S(1)} %get-tuple-element.159, u32[4096]{0:T(1024)S(1)} %broadcast_clamp_fusion.2), kind=kCustom, calls=%fused_computation.clone.clone.1 | custom fusion | bytes 49152 | tf_op jit(solution)/shard_map/jit(searchsorted)/jit(_searchsorted_scan_impl)/vmap(jit(_searchsorted_scan_impl))/while/body/eval_jaxpr/gather | solution.py:68
  377.3 23.0 %gather_fusion = s32[4096]{0:T(1024)S(1)} fusion(s32[2048]{0:T(1024)S(1)} %get-tuple-element.159, u32[4096]{0:T(1024)S(1)} %broadcast_clamp_fusion.2), kind=kCustom, calls=%fused_computation.clone.clone.1 | custom fusion | bytes 49152 | tf_op jit(solution)/shard_map/jit(searchsorted)/jit(_searchsorted_scan_impl)/vmap(jit(_searchsorted_scan_impl))/while/body/eval_jaxpr/gather | solution.py:68
  400.5 23.0 %gather_fusion = s32[4096]{0:T(1024)S(1)} fusion(s32[2048]{0:T(1024)S(1)} %get-tuple-element.159, u32[4096]{0:T(1024)S(1)} %broadcast_clamp_fusion.2), kind=kCustom, calls=%fused_computation.clone.clone.1 | custom fusion | bytes 49152 | tf_op jit(solution)/shard_map/jit(searchsorted)/jit(_searchsorted_scan_impl)/vmap(jit(_searchsorted_scan_impl))/while/body/eval_jaxpr/gather | solution.py:68
  423.6 23.0 %gather_fusion = s32[4096]{0:T(1024)S(1)} fusion(s32[2048]{0:T(1024)S(1)} %get-tuple-element.159, u32[4096]{0:T(1024)S(1)} %broadcast_clamp_fusion.2), kind=kCustom, calls=%fused_computation.clone.clone.1 | custom fusion | bytes 49152 | tf_op jit(solution)/shard_map/jit(searchsorted)/jit(_searchsorted_scan_impl)/vmap(jit(_searchsorted_scan_impl))/while/body/eval_jaxpr/gather | solution.py:68
  446.7 23.0 %gather_fusion = s32[4096]{0:T(1024)S(1)} fusion(s32[2048]{0:T(1024)S(1)} %get-tuple-element.159, u32[4096]{0:T(1024)S(1)} %broadcast_clamp_fusion.2), kind=kCustom, calls=%fused_computation.clone.clone.1 | custom fusion | bytes 49152 | tf_op jit(solution)/shard_map/jit(searchsorted)/jit(_searchsorted_scan_impl)/vmap(jit(_searchsorted_scan_impl))/while/body/eval_jaxpr/gather | solution.py:68
  469.9 23.0 %gather_fusion = s32[4096]{0:T(1024)S(1)} fusion(s32[2048]{0:T(1024)S(1)} %get-tuple-element.159, u32[4096]{0:T(1024)S(1)} %broadcast_clamp_fusion.2), kind=kCustom, calls=%fused_computation.clone.clone.1 | custom fusion | bytes 49152 | tf_op jit(solution)/shard_map/jit(searchsorted)/jit(_searchsorted_scan_impl)/vmap(jit(_searchsorted_scan_impl))/while/body/eval_jaxpr/gather | solution.py:68
  493.0 23.0 %gather_fusion = s32[4096]{0:T(1024)S(1)} fusion(s32[2048]{0:T(1024)S(1)} %get-tuple-element.159, u32[4096]{0:T(1024)S(1)} %broadcast_clamp_fusion.2), kind=kCustom, calls=%fused_computation.clone.clone.1 | custom fusion | bytes 49152 | tf_op jit(solution)/shard_map/jit(searchsorted)/jit(_searchsorted_scan_impl)/vmap(jit(_searchsorted_scan_impl))/while/body/eval_jaxpr/gather | solution.py:68
  516.1 23.0 %gather_fusion = s32[4096]{0:T(1024)S(1)} fusion(s32[2048]{0:T(1024)S(1)} %get-tuple-element.159, u32[4096]{0:T(1024)S(1)} %broadcast_clamp_fusion.2), kind=kCustom, calls=%fused_computation.clone.clone.1 | custom fusion | bytes 49152 | tf_op jit(solution)/shard_map/jit(searchsorted)/jit(_searchsorted_scan_impl)/vmap(jit(_searchsorted_scan_impl))/while/body/eval_jaxpr/gather | solution.py:68
  539.2 23.0 %gather_fusion = s32[4096]{0:T(1024)S(1)} fusion(s32[2048]{0:T(1024)S(1)} %get-tuple-element.159, u32[4096]{0:T(1024)S(1)} %broadcast_clamp_fusion.2), kind=kCustom, calls=%fused_computation.clone.clone.1 | custom fusion | bytes 49152 | tf_op jit(solution)/shard_map/jit(searchsorted)/jit(_searchsorted_scan_impl)/vmap(jit(_searchsorted_scan_impl))/while/body/eval_jaxpr/gather | solution.py:68
  562.4 9.2 %reduce-window.21 = s32[32,32,128]{2,1,0:T(8,128)S(1)} reduce-window(s32[32,32,128]{2,1,0:T(8,128)S(1)} %fusion.16, s32[]{:T(128)} %constant.89.clone.1), window={size=1x1x128 pad=0_0x0_0x127_0}, to_apply=%region_0.0 | reduce-window | flops 16646144 | bytes 1048580 | tf_op jit(solution)/shard_map/reduce-window
  571.7 0.8 slice_reduce_fusion
  572.8 0.4 fusion.15
  573.3 15.5 %scatter_custom_fusion = s32[4096]{0:T(1024)S(1)} fusion(s32[4096]{0:T(1024)S(1)} %get-tuple-element.103, s32[4096]{0:T(1024)S(1)} %get-tuple-element.101, s32[]{:T(128)} %constant.89.clone.1), kind=kCustom, calls=%fused_computation.59 | custom fusion | bytes 16388 | tf_op jit(solution)/shard_map/scatter | solution.py:87
  588.8 41.8 %scatter_custom_fusion.1 = bf16[4096,512]{1,0:T(8,128)(2,1)} fusion(s32[4096]{0:T(1024)S(1)} %get-tuple-element.103, f32[4096]{0:T(1024)S(1)} %broadcast_multiply_fusion, f32[]{:T(128)} %constant.106.clone.1, f32[]{:T(128)} %constant.105.clone.1, f32[4096]{0:T(1024)S(1)} %copy-done.1, f32[4096]{0:T(1024)S(1)} %copy-done.2, bf16[]{:T(256)} %constant.96.clone.1, ...), kind=kCustom, calls=%fused_computation.11 | custom fusion | flops 14680064 | bytes 6357002 | tf_op jit(solution)/shard_map/scatter | solution.py:81
  630.7 6.6 fusion.10
  637.3 154.7 %reduce-scatter.5.cloned.1.call-done = f32[128,512]{1,0:T(8,128)} async-done(((f32[4096,512]{1,0:T(8,128)}), f32[128,512]{1,0:T(8,128)}) %reduce-scatter.5.cloned.1.call-update) | async-done | bytes 262160 | tf_op jit(solution)/shard_map/reduce_scatter | solution.py:95
  (98 shorter events, 2.8 us)
Async XLA Ops:
  6.5 58.0 %all-gather.2.cloned.1.call-start = ((), (), s32[]{:S(2)}) async-start(), calls=%async_computation.3 | async-start | bytes 5242880 | tf_op jit(solution)/shard_map/all_gather | solution.py:29
  7.3 268.6 %reduce-scatter.3.cloned.1.call-start = ((), (), s32[]{:S(2)}) async-start(), calls=%async_computation.4 | async-start | bytes 18874368 | tf_op jit(solution)/shard_map/reduce_scatter | solution.py:30
  107.6 0.9 copy-start
  107.6 14.4 %copy-start.4 = (s32[4096]{0:T(1024)S(1)}, s32[4096]{0:T(1024)}, u32[]{:S(2)}) copy-start(s32[4096]{0:T(1024)} %param.15) | copy-start | bytes 49156
  107.6 168.3 %copy-start.6 = (f32[1024]{0:T(1024)S(1)}, f32[1024]{0:T(1024)}, u32[]{:S(2)}) copy-start(f32[1024]{0:T(1024)} %param.13) | copy-start | bytes 12292
  281.3 307.6 %all-to-all-start = ((bf16[32,64,512]{2,1,0:T(8,128)(2,1)}), bf16[32,64,512]{2,1,0:T(8,128)(2,1)S(1)}, u32[]{:S(2)}, u32[]{:S(2)}) async-start(bf16[32,64,512]{2,1,0:T(8,128)(2,1)} %bitcast.56), calls=%async_computation.1 | async-start | bytes 4194304 | tf_op jit(solution)/shard_map/all_to_all | solution.py:57
  284.5 507.5 %reduce-scatter.5.cloned.1.call-start = ((), (), s32[]{:S(2)}) async-start(), calls=%async_computation.5 | async-start | bytes 8650752 | tf_op jit(solution)/shard_map/reduce_scatter | solution.py:95
  284.8 277.6 %copy-start.3 = (s32[4096]{0:T(1024)S(1)}, s32[4096]{0:T(1024)}, u32[]{:S(2)}) copy-start(s32[4096]{0:T(1024)} %param.16) | copy-start | bytes 49156
  284.8 304.0 %copy-start.5 = (f32[4096]{0:T(1024)S(1)}, f32[4096]{0:T(1024)}, u32[]{:S(2)}) copy-start(f32[4096]{0:T(1024)} %param.19) | copy-start | bytes 49156
  284.8 304.0 %copy-start.1 = (f32[4096]{0:T(1024)S(1)}, f32[4096]{0:T(1024)}, u32[]{:S(2)}) copy-start(f32[4096]{0:T(1024)} %param.18) | copy-start | bytes 49156
  284.8 304.0 %copy-start.2 = (f32[4096]{0:T(1024)S(1)}, f32[4096]{0:T(1024)}, u32[]{:S(2)}) copy-start(f32[4096]{0:T(1024)} %param.17) | copy-start | bytes 49156
Sparse Core Ops, SparseCore 0:
  9.2 55.2 all-gather.1
  107.8 168.0 reduce-scatter.2
  637.5 154.5 reduce-scatter.4
where the time goes:
time: 799 us
  waiting for transfers between devices  366 us (46%)
  local copies, waits for them, and re-layouts  295 us (37%)
  other arithmetic  63.2 us (8%)
  matrix products  55.1 us (7%)
  between operations  14.6 us (2%)
    gather x12, local copies, waits for them, and re-layouts, per_device(): slot_index = jnp.searchsorted(running, chosen + 1, side='left')  276 us
    reduce_scatter x1, waiting for transfers between devices, per_device(): lax.psum_scatter(zone_table, ('row', 'col'), scatter_dimension=0, tiled=T...  155 us
    reduce_scatter x1, waiting for transfers between devices, per_device(): lax.psum_scatter(lax.dot_general(chol_factor, panel_rows, (((1,), (1,)),...  154 us
    all_gather x1, waiting for transfers between devices, per_device(): panel_rows = lax.all_gather(normals, 'row', axis=0, tiled=True)  57.2 us
    dot_general x1, matrix products, per_device(): lax.dot_general(chol_factor, panel_rows, (((1,), (1,)), ((), ())), prefer...  43.1 us
    scatter x1, other arithmetic, per_device(): jnp.zeros_like(damage).at[placing].set(damage)  41.8 us
    another operation x9, other arithmetic  19.2 us
  transfers between devices with their start and end apart: 4, of which 3 were waited for; matrix products, arithmetic and copies ran while one was open for 40% of the time, Pallas kernels for 0%

commit v1 on v0

v1 whole, which is shorter than its diff:
```python
import jax
import jax.numpy as jnp
from jax import lax
from jax.experimental import pallas as pl
from jax.experimental.pallas import tpu as pltpu
from jax.sharding import PartitionSpec as P

ZONES = 4096
CHUNKS = 2


def normal_cdf(argument):
    return 0.5 * (1.0 + jax.scipy.special.erf(argument * 0.7071067811865476))


def swap(value, axis, bit):
    size = lax.axis_size(axis)
    return lax.ppermute(value, axis, [(i, i ^ bit) for i in range(size)])


def bits_of(size):
    return [1 << k for k in range(size.bit_length() - 1)]


def gather_rows(block, order):
    me = lax.axis_index("row")
    held = block
    axes = []
    for bit in order:
        other = swap(held, "row", bit)
        low = (me // bit) % 2 == 0
        held = jnp.stack([jnp.where(low, held, other), jnp.where(low, other, held)], axis=0)
        axes.insert(0, bit)
    rank = [axes.index(bit) for bit in sorted(axes, reverse=True)]
    held = held.transpose(tuple(rank) + (len(axes), len(axes) + 1))
    return held.reshape(-1, block.shape[1])


def panel_kernel(side_ref, factor_ref, *refs):
    count = len(refs) // 2
    for panel_ref, out_ref in zip(refs[:count], refs[count:]):
        out_ref[...] = lax.dot_general(
            factor_ref[...],
            panel_ref[...],
            (((1,), (1,)), ((), ())),
            preferred_element_type=jnp.float32,
        ).astype(out_ref.dtype)


def half_field(chol_factor, panels, side, line, block, dtype):
    depth = chol_factor.shape[1]
    tile = min(512, block)
    per_block = block // tile
    panel_specs = [pl.BlockSpec(p.shape, lambda i, j, side: (0, 0)) for p in panels]
    out_specs = [
        pl.BlockSpec((tile, p.shape[0]), lambda i, j, side: (i * per_block + j, 0))
        for p in panels
    ]
    rows = line * block
    events = sum(p.shape[0] for p in panels)
    return pl.pallas_call(
        panel_kernel,
        grid_spec=pltpu.PrefetchScalarGridSpec(
            num_scalar_prefetch=1,
            grid=(line, per_block),
            in_specs=[
                pl.BlockSpec(
                    (tile, depth),
                    lambda i, j, side: ((2 * i + side[0]) * per_block + j, 0),
                )
            ]
            + panel_specs,
            out_specs=out_specs,
        ),
        out_shape=[jax.ShapeDtypeStruct((rows, p.shape[0]), dtype) for p in panels],
        compiler_params=pltpu.CompilerParams(vmem_limit_bytes=48 * 1024 * 1024),
        cost_estimate=pl.CostEstimate(
            flops=2 * rows * depth * events,
            bytes_accessed=2 * rows * depth + 4 * rows * events,
            transcendentals=0,
        ),
    )(side.reshape(1).astype(jnp.int32), chol_factor, *panels)


def field_scatter(mine, theirs):
    me = lax.axis_index("col")
    line = mine.shape[0]
    place = me // 2
    summed = mine + swap(theirs, "col", 1).astype(jnp.float32)
    up = down = None
    for step in range(1, line):
        index_up = jnp.clip(place + line - step, 0, line - 1)
        index_down = jnp.clip(place - line + step, 0, line - 1)
        send_up = lax.dynamic_index_in_dim(summed, index_up, 0, keepdims=False)
        send_down = lax.dynamic_index_in_dim(summed, index_down, 0, keepdims=False)
        if up is not None:
            send_up = send_up + up.astype(jnp.float32)
            send_down = send_down + down.astype(jnp.float32)
        pairs_up, pairs_down = [], []
        for p in range(line):
            for c in range(2):
                if p < step and p + 1 < line:
                    pairs_up.append((2 * p + c, 2 * p + 2 + c))
                if p >= line - step and p > 0:
                    pairs_down.append((2 * p + c, 2 * p - 2 + c))
        up = lax.ppermute(send_up.astype(jnp.bfloat16), "col", pairs_up)
        down = lax.ppermute(send_down.astype(jnp.bfloat16), "col", pairs_down)
    own = lax.dynamic_index_in_dim(summed, place, 0, keepdims=False)
    if up is not None:
        own = own + up.astype(jnp.float32) + down.astype(jnp.float32)
    return own


def zone_scatter(table, order):
    rows, cols = lax.axis_size("row"), lax.axis_size("col")
    dims = [2] * (len(bits_of(rows)) + len(bits_of(cols)))
    row_bits, col_bits = bits_of(rows), bits_of(cols)
    tail = table.shape[1:]
    steps = [("col", 1)] + [("row", b) for b in order] + [("col", b) for b in col_bits[:0:-1]]
    names = [("row", b) for b in row_bits[::-1]] + [("col", b) for b in col_bits[::-1]]
    held = table.reshape(tuple(dims) + tail)
    for number, (axis, bit) in enumerate(steps):
        where = names.index((axis, bit))
        names.pop(where)
        side = (lax.axis_index(axis) // bit) % 2
        give = lax.dynamic_index_in_dim(held, 1 - side, where, keepdims=False)
        keep = lax.dynamic_index_in_dim(held, side, where, keepdims=False)
        if number < len(steps) - 1:
            give = give.astype(jnp.bfloat16)
        held = keep + swap(give, axis, bit).astype(jnp.float32)
    return held


def split3(value):
    high = lax.reduce_precision(value, 8, 7)
    rest = value - high
    middle = lax.reduce_precision(rest, 8, 7)
    return [high, middle, rest - middle]


def per_device(
    chol_factor,
    normals,
    site_median,
    site_region,
    asset_pick,
    asset_zone,
    asset_capacity,
    asset_beta,
    asset_value,
):
    rows, cols = lax.axis_size("row"), lax.axis_size("col")
    device_count = rows * cols
    own_index = lax.axis_index(("row", "col"))
    local_events = normals.shape[0]
    part = local_events // CHUNKS
    row_bits = bits_of(rows)

    gathered = []
    for chunk in range(CHUNKS):
        order = row_bits if chunk % 2 == 0 else row_bits[::-1]
        gathered.append(gather_rows(normals[chunk * part : (chunk + 1) * part], order))

    site_count = site_median.shape[0]
    slot_cap = max(2, 2 * site_count // device_count)
    slots = device_count * slot_cap
    all_regions = site_region[:, 0].reshape(device_count, site_count)
    block_regions = lax.dynamic_index_in_dim(all_regions, own_index, 0, keepdims=False)
    devices = jnp.arange(device_count, dtype=jnp.int32)

    def rank_of(labels):
        count = labels.shape[0]
        steps = jnp.arange(count, dtype=jnp.int32)
        onehot = (labels[:, None] == devices[None, :]).astype(jnp.bfloat16)
        before = (steps[:, None] > steps[None, :]).astype(jnp.bfloat16)
        running = jnp.dot(before, onehot, preferred_element_type=jnp.float32)
        return jnp.sum(running * onehot.astype(jnp.float32), axis=1).astype(jnp.int32)

    position = block_regions * slot_cap + rank_of(block_regions)
    selector = (position[None, :] == jnp.arange(slots, dtype=jnp.int32)[:, None]).astype(
        jnp.bfloat16
    )
    counts = jnp.sum((all_regions == own_index).astype(jnp.int32), axis=1)
    first = jnp.sum(jnp.where(devices[None, :] < devices[:, None], counts[None, :], 0), axis=1)
    slot_steps = jnp.arange(slot_cap, dtype=jnp.int32)[None, :]
    slot_rank = jnp.where(
        slot_steps < counts[:, None], first[:, None] + slot_steps, -1
    ).reshape(-1)
    total = jnp.sum(counts)

    assets = asset_pick.shape[0]
    zone_share = ZONES // device_count
    per_owner = assets // device_count
    zone_owner = asset_zone // zone_share
    placing = zone_owner * per_owner + rank_of(zone_owner)
    chosen = asset_pick % total
    table = jnp.stack(
        split3(asset_capacity)
        + split3(asset_beta)
        + split3(asset_value)
        + [
            (chosen // 256).astype(jnp.float32),
            (chosen % 256).astype(jnp.float32),
            (asset_zone % zone_share).astype(jnp.float32),
        ],
        axis=1,
    ).astype(jnp.bfloat16)
    order_of = (placing[None, :] == jnp.arange(assets, dtype=jnp.int32)[:, None]).astype(
        jnp.bfloat16
    )
    placed = jnp.dot(order_of, table, preferred_element_type=jnp.float32)
    capacity = placed[:, 0] + placed[:, 1] + placed[:, 2]
    beta = placed[:, 3] + placed[:, 4] + placed[:, 5]
    value = placed[:, 6] + placed[:, 7] + placed[:, 8]
    pick = (placed[:, 9] * 256.0 + placed[:, 10]).astype(jnp.int32)
    inner_zone = placed[:, 11].astype(jnp.int32).reshape(device_count, per_owner)
    member = (
        inner_zone[:, None, :] == jnp.arange(zone_share, dtype=jnp.int32)[None, :, None]
    ).astype(jnp.bfloat16)
    chooser = (pick[:, None] == slot_rank[None, :]).astype(jnp.bfloat16)

    line, core = cols // 2, lax.axis_index("col") % 2
    theirs = half_field(chol_factor, gathered, 1 - core, line, site_count, jnp.bfloat16)
    mine = half_field(chol_factor, gathered, core, line, site_count, jnp.float32)

    results = []
    for chunk in range(CHUNKS):
        shape = (line, site_count, rows * part)
        field = field_scatter(mine[chunk].reshape(shape), theirs[chunk].reshape(shape))
        log_motion = (site_median[:, None] + field).astype(jnp.bfloat16)
        events = log_motion.shape[1]
        outgoing = jnp.dot(selector, log_motion, preferred_element_type=jnp.float32).astype(
            jnp.bfloat16
        )
        incoming = lax.all_to_all(
            outgoing.reshape(device_count, slot_cap, events),
            ("row", "col"),
            split_axis=0,
            concat_axis=0,
            tiled=True,
        ).reshape(slots, events)
        motion = jnp.dot(chooser, incoming, preferred_element_type=jnp.float32)
        damage = (
            value[:, None] * normal_cdf((motion - capacity[:, None]) / beta[:, None])
        ).astype(jnp.bfloat16)
        zone_table = jnp.einsum(
            "dzp,dpe->dze",
            member,
            damage.reshape(device_count, per_owner, events),
            preferred_element_type=jnp.float32,
        )
        order = row_bits if chunk % 2 == 0 else row_bits[::-1]
        zones = zone_scatter(zone_table, order)
        results.append(zones.reshape(zone_share, rows, part))
    return jnp.stack(results, axis=2).reshape(zone_share, rows * local_events)


def solution(mesh):
    in_specs = (
        P("row", "col"),
        P("row", "col"),
        P(("row", "col")),
        P(),
        P(("row", "col")),
        P(("row", "col")),
        P(("row", "col")),
        P(("row", "col")),
        P(("row", "col")),
    )
    out_specs = P(("row", "col"), None)
    return jax.shard_map(
        per_device, mesh=mesh, in_specs=in_specs, out_specs=out_specs, check_vma=False
    )
```

time: 799 us -> 314 us (0.39)
  local copies, waits for them, and re-layouts: 295 us -> 15.6 us
  waiting for transfers between devices: 366 us -> 123 us
  Pallas kernels: 0 us -> 47.2 us
  starting transfers between devices: 3.52 us -> 48 us
  other arithmetic: 63.2 us -> 24.7 us
  between operations: 14.6 us -> 2.16 us
    reduce_scatter x2 -> x0, waiting for transfers between devices: 308 us -> none  [the longest x1 155 us: per_device(): lax.psum_scatter(zone_table, ('row', 'col'), scatter_dimension=0, tiled=T...]
    gather x12 -> x0, local copies, waits for them, and re-layouts: 276 us -> none  [per_device(): slot_index = jnp.searchsorted(running, chosen + 1, side='left')]
    ppermute x0 -> x28, waiting for transfers between devices: none -> 106 us  [the longest x16 63 us: swap(): return lax.ppermute(value, axis, [(i, i ^ bit) for i in range(size)])]
    all_gather x1 -> x0, waiting for transfers between devices: 57.2 us -> none  [per_device(): panel_rows = lax.all_gather(normals, 'row', axis=0, tiled=True)]
    pallas_call x0 -> x2, Pallas kernels: none -> 47.2 us  [half_field(): pl.pallas_call(panel_kernel, grid_spec=pltpu.PrefetchScalarGridSpec(num_s...]
    scatter x1 -> x0, other arithmetic: 41.8 us -> none  [per_device(): jnp.zeros_like(damage).at[placing].set(damage)]
    ppermute x0 -> x28, starting transfers between devices: none -> 37.8 us  [the longest x6 19.2 us: field_scatter(): up = lax.ppermute(send_up.astype(jnp.bfloat16), 'col', pairs_up)]
    all_to_all x1 -> x2, waiting for transfers between devices: 0.01 us -> 17 us  [per_device(): lax.all_to_all(outgoing.reshape(device_count, slot_cap, events), ('row',...]
  transfers between devices with their start and end apart: 4 -> 30, of which waited for: 3 -> 19; matrix products, arithmetic and copies ran while one was open for 40% -> 24% of each run, Pallas kernels for 0% -> 7%
where the time goes in v1:
time: 314 us; the launch traced here: 313 us
  waiting for transfers between devices  123 us (39%)
  matrix products  52 us (17%)
  starting transfers between devices  48 us (15%)
  Pallas kernels  47.2 us (15%)
  other arithmetic  24.7 us (8%)
  local copies, waits for them, and re-layouts  15.6 us (5%)
    ppermute x16, waiting for transfers between devices, swap(): return lax.ppermute(value, axis, [(i, i ^ bit) for i in range(size)])  63 us
    pallas_call x2, Pallas kernels, half_field(): pl.pallas_call(panel_kernel, grid_spec=pltpu.PrefetchScalarGridSpec(num_s...  47.2 us
    ppermute x6, waiting for transfers between devices, field_scatter(): up = lax.ppermute(send_up.astype(jnp.bfloat16), 'col', pairs_up)  37.8 us
    ppermute x6, starting transfers between devices, field_scatter(): up = lax.ppermute(send_up.astype(jnp.bfloat16), 'col', pairs_up)  19.2 us
    dot_general x2, matrix products, rank_of(): running = jnp.dot(before, onehot, preferred_element_type=jnp.float32)  17.6 us
    all_to_all x2, waiting for transfers between devices, per_device(): lax.all_to_all(outgoing.reshape(device_count, slot_cap, events), ('row',...  17 us
    dot_general x2, matrix products, per_device(): motion = jnp.dot(chooser, incoming, preferred_element_type=jnp.float32)  14.3 us
    ppermute x16, starting transfers between devices, swap(): return lax.ppermute(value, axis, [(i, i ^ bit) for i in range(size)])  12.4 us
  transfers between devices with their start and end apart: 30, of which 19 were waited for; matrix products, arithmetic and copies ran while one was open for 24% of the time, Pallas kernels for 7%

profile of v1, /device:TPU:0, one launch (start us, length us, event | category | flops | bytes accessed | tf_op | source)
XLA Modules:
  0.0 313.2 jit_solution(10055310572853236756)
XLA Ops:
  1.3 3.0 collective-permute-start
  5.8 10.4 %collective-permute-done = bf16[64,4096]{1,0:T(8,128)(2,1)S(1)} collective-permute-done((bf16[64,4096]{1,0:T(8,128)(2,1)S(1)}, bf16[64,4096]{1,0:T(8,128)(2,1)S(1)}, u32[]{:S(2)}, u32[]{:S(2)}) %collective-permute-start) | collective-permute-done | bytes 524320 | tf_op jit(solution)/shard_map/ppermute | solution.py:18
  27.1 16.9 %collective-permute-done.1 = bf16[2,64,4096]{2,1,0:T(8,128)(2,1)S(1)} collective-permute-done((bf16[2,64,4096]{2,1,0:T(8,128)(2,1)}, bf16[2,64,4096]{2,1,0:T(8,128)(2,1)S(1)}, u32[]{:S(2)}, u32[]{:S(2)}) %collective-permute-start.1) | collective-permute-done | bytes 1048608 | tf_op jit(solution)/shard_map/ppermute | solution.py:18
  44.1 2.4 collective-permute-done.3
  51.2 24.3 %shard_map.92 = (bf16[4096,256]{1,0:T(8,128)(2,1)}, bf16[4096,256]{1,0:T(8,128)(2,1)S(1)}) custom-call(s32[1]{0:T(128)} %bitcast.18.side_ref, bf16[8192,4096]{1,0:T(8,128)(2,1)} %factor_ref.3, bf16[256,4096]{1,0:T(8,128)(2,1)} %bitcast.149, bf16[256,4096]{1,0:T(8,128)(2,1)} %bitcast.147), custom_call_target="tpu_custom_call" | custom-call | flops 17179869184 | bytes 41943040 | tf_op jit(solution)/shard_map/pallas_call | solution.py:61
  79.6 22.9 %shard_map.91 = (f32[4096,256]{1,0:T(8,128)}, f32[4096,256]{1,0:T(8,128)}) custom-call(s32[1]{0:T(128)} %bitcast.5.side_ref, bf16[8192,4096]{1,0:T(8,128)(2,1)} %factor_ref.3, bf16[256,4096]{1,0:T(8,128)(2,1)S(1)} %bitcast.150, bf16[256,4096]{1,0:T(8,128)(2,1)S(1)} %bitcast.148), custom_call_target="tpu_custom_call" | custom-call | flops 17179869184 | bytes 41943040 | tf_op jit(solution)/shard_map/pallas_call | solution.py:61
  102.5 3.3 %convert_add_fusion.1 = f32[4,1024,256]{2,1,0:T(8,128)S(1)} fusion(f32[4,1024,256]{2,1,0:T(8,128)} %bitcast.157, bf16[4,1024,256]{2,1,0:T(8,128)(2,1)} %collective-permute-done.4), kind=kLoop, calls=%fused_computation.32 | loop fusion | flops 2097152 | bytes 10485760 | tf_op jit(solution)/shard_map/add | solution.py:89
  105.9 3.5 %collective-permute-start.5 = (bf16[1024,256]{1,0:T(8,128)(2,1)S(1)}, bf16[1024,256]{1,0:T(8,128)(2,1)S(1)}, u32[]{:S(2)}, u32[]{:S(2)}) collective-permute-start(bf16[1024,256]{1,0:T(8,128)(2,1)S(1)} %get-tuple-element.17), channel_id=1, source_target_pairs={{0,2},{1,3},{8,10},{9,11},{16,18},{17,19},{24,26},{25,27}} | collective-permute-start | bytes 1572872 | tf_op jit(solution)/shard_map/ppermute | solution.py:106
  109.5 17.1 %fusion.63 = f32[4096]{0:T(1024)S(1)} fusion(s32[4096]{0:T(1024)S(1)} %add_select_fusion.4), kind=kOutput, calls=%fused_computation.48 | convolution fusion | flops 1091301376 | bytes 32768 | tf_op jit(solution)/shard_map/dot_general | solution.py:176
  132.4 3.4 %collective-permute-start.17 = (bf16[1024,256]{1,0:T(8,128)(2,1)}, bf16[1024,256]{1,0:T(8,128)(2,1)S(1)}, u32[]{:S(2)}, u32[]{:S(2)}) collective-permute-start(bf16[1024,256]{1,0:T(8,128)(2,1)} %get-tuple-element.21), channel_id=1, source_target_pairs={{0,2},{1,3},{8,10},{9,11},{16,18},{17,19},{24,26},{25,27}} | collective-permute-start | bytes 1572872 | tf_op jit(solution)/shard_map/ppermute | solution.py:106
  135.9 5.1 %collective-permute-done.6 = bf16[1024,256]{1,0:T(8,128)(2,1)S(1)} collective-permute-done((bf16[1024,256]{1,0:T(8,128)(2,1)S(1)}, bf16[1024,256]{1,0:T(8,128)(2,1)S(1)}, u32[]{:S(2)}, u32[]{:S(2)}) %collective-permute-start.6) | collective-permute-done | bytes 524320 | tf_op jit(solution)/shard_map/ppermute | solution.py:106
  143.7 7.7 %collective-permute-done.17 = bf16[1024,256]{1,0:T(8,128)(2,1)S(1)} collective-permute-done((bf16[1024,256]{1,0:T(8,128)(2,1)}, bf16[1024,256]{1,0:T(8,128)(2,1)S(1)}, u32[]{:S(2)}, u32[]{:S(2)}) %collective-permute-start.17) | collective-permute-done | bytes 524320 | tf_op jit(solution)/shard_map/ppermute | solution.py:106
  152.8 4.5 %collective-permute-start.18 = (bf16[1024,256]{1,0:T(8,128)(2,1)S(1)}, bf16[1024,256]{1,0:T(8,128)(2,1)S(1)}, u32[]{:S(2)}, u32[]{:S(2)}) collective-permute-start(bf16[1024,256]{1,0:T(8,128)(2,1)S(1)} %fusion.70), channel_id=1, source_target_pairs={{0,2},{1,3},{2,4},{3,5},{8,10},{9,11},{10,12},{11,13},{16,18},{17,... | collective-permute-start | bytes 1572872 | tf_op jit(solution)/shard_map/ppermute | solution.py:106
  157.3 2.7 collective-permute-start.7
  163.5 6.0 %collective-permute-done.18 = bf16[1024,256]{1,0:T(8,128)(2,1)S(1)} collective-permute-done((bf16[1024,256]{1,0:T(8,128)(2,1)S(1)}, bf16[1024,256]{1,0:T(8,128)(2,1)S(1)}, u32[]{:S(2)}, u32[]{:S(2)}) %collective-permute-start.18) | collective-permute-done | bytes 524320 | tf_op jit(solution)/shard_map/ppermute | solution.py:106
  172.0 7.0 %collective-permute-done.7 = bf16[1024,256]{1,0:T(8,128)(2,1)} collective-permute-done((bf16[1024,256]{1,0:T(8,128)(2,1)S(1)}, bf16[1024,256]{1,0:T(8,128)(2,1)}, u32[]{:S(2)}, u32[]{:S(2)}) %collective-permute-start.7) | collective-permute-done | bytes 524320 | tf_op jit(solution)/shard_map/ppermute | solution.py:106
  179.1 4.3 %fusion.59 = bf16[2048,256]{1,0:T(8,128)(2,1)} fusion(s32[1024]{0:T(1024)S(1)} %bitcast.178, bf16[1024,256]{1,0:T(8,128)(2,1)} %collective-permute-done.10, bf16[1024,256]{1,0:T(8,128)(2,1)} %collective-permute-done.7, f32[4,1024,256]{2,1,0:T(8,128)} %copy-done.5, s32[]{:T(128)S(6)} %select_n.245, f32[1024]{0:T(1024)S(1)} %copy-done.17), kind=kOutput, calls=%fused_computation.37 | convolution fusion | flops 1077936128 | bytes 3153924 | tf_op jit(solution)/shard_map/dot_general | solution.py:232
  183.3 4.4 %all-to-all-start = ((bf16[32,64,256]{2,1,0:T(8,128)(2,1)}), bf16[32,64,256]{2,1,0:T(8,128)(2,1)S(1)}, u32[]{:S(2)}, u32[]{:S(2)}) async-start(bf16[32,64,256]{2,1,0:T(8,128)(2,1)} %bitcast.27), calls=%async_computation | async-start | bytes 2097152 | tf_op jit(solution)/shard_map/all_to_all | solution.py:235
  187.8 11.7 %fusion.1 = f32[4096,12]{0,1:T(8,128)S(1)} fusion(bf16[4096,12]{0,1:T(8,128)(2,1)S(1)} %stack.103, s32[4096]{0:T(1024)S(1)} %get-tuple-element.44), kind=kOutput, calls=%fused_computation.3 | convolution fusion | flops 419430400 | bytes 311296 | tf_op jit(solution)/shard_map/dot_general | solution.py:211
  199.5 3.7 %collective-permute-start.19 = (bf16[1024,256]{1,0:T(8,128)(2,1)S(1)}, bf16[1024,256]{1,0:T(8,128)(2,1)S(1)}, u32[]{:S(2)}, u32[]{:S(2)}) collective-permute-start(bf16[1024,256]{1,0:T(8,128)(2,1)S(1)} %get-tuple-element.19), channel_id=1, source_target_pairs={{0,2},{1,3},{2,4},{3,5},{4,6},{5,7},{8,10},{9,11},{10,12},{11,13},... | collective-permute-start | bytes 1572872 | tf_op jit(solution)/shard_map/ppermute | solution.py:106
  204.8 11.8 %collective-permute-done.19 = bf16[1024,256]{1,0:T(8,128)(2,1)S(1)} collective-permute-done((bf16[1024,256]{1,0:T(8,128)(2,1)S(1)}, bf16[1024,256]{1,0:T(8,128)(2,1)S(1)}, u32[]{:S(2)}, u32[]{:S(2)}) %collective-permute-start.19) | collective-permute-done | bytes 524320 | tf_op jit(solution)/shard_map/ppermute | solution.py:106
  216.6 5.8 %collective-permute-done.22 = bf16[1024,256]{1,0:T(8,128)(2,1)S(1)} collective-permute-done((bf16[1024,256]{1,0:T(8,128)(2,1)S(1)}, bf16[1024,256]{1,0:T(8,128)(2,1)S(1)}, u32[]{:S(2)}, u32[]{:S(2)}) %collective-permute-start.22) | collective-permute-done | bytes 524320 | tf_op jit(solution)/shard_map/ppermute | solution.py:107
  222.4 2.8 fusion.60
  225.1 5.8 %all-to-all-start.1 = ((bf16[32,64,256]{2,1,0:T(8,128)(2,1)}), bf16[32,64,256]{2,1,0:T(8,128)(2,1)S(1)}, u32[]{:S(2)}, u32[]{:S(2)}) async-start(bf16[32,64,256]{2,1,0:T(8,128)(2,1)} %bitcast.54), calls=%async_computation.1 | async-start | bytes 2097152 | tf_op jit(solution)/shard_map/all_to_all | solution.py:235
  231.1 7.1 %fusion.52 = bf16[4096,256]{1,0:T(8,128)(2,1)S(1)} fusion(bf16[2048,256]{1,0:T(8,128)(2,1)S(1)} %bitcast.160, s32[2048]{0:T(1024)S(1)} %select_n.226, s32[4096]{0:T(1024)S(1)} %bitcast.173, f32[4096]{0:T(1024)S(1)} %bitcast.169, f32[4096]{0:T(1024)S(1)} %bitcast.171, f32[4096]{0:T(1024)S(1)} %bitcast.175), kind=kOutput, calls=%fused_computation.29 | convolution fusion | flops 4309647360 | bytes 3219456 | tf_op jit(solution)/shard_map/dot_general | solution.py:242
  241.2 17.0 %all-to-all-done.1 = bf16[32,64,256]{2,1,0:T(8,128)(2,1)S(1)} async-done(((bf16[32,64,256]{2,1,0:T(8,128)(2,1)}), bf16[32,64,256]{2,1,0:T(8,128)(2,1)S(1)}, u32[]{:S(2)}, u32[]{:S(2)}) %all-to-all-start.1) | async-done | bytes 1048608 | tf_op jit(solution)/shard_map/all_to_all | solution.py:235
  258.2 7.1 %fusion.34 = bf16[4096,256]{1,0:T(8,128)(2,1)S(1)} fusion(bf16[2048,256]{1,0:T(8,128)(2,1)S(1)} %bitcast.161, s32[2048]{0:T(1024)S(1)} %select_n.226, s32[4096]{0:T(1024)S(1)} %bitcast.174, f32[4096]{0:T(1024)S(1)} %bitcast.170, f32[4096]{0:T(1024)S(1)} %bitcast.172, f32[4096]{0:T(1024)S(1)} %bitcast.176), kind=kOutput, calls=%fused_computation.23 | convolution fusion | flops 4309647360 | bytes 3219456 | tf_op jit(solution)/shard_map/dot_general | solution.py:242
  273.7 11.1 %collective-permute-done.12 = bf16[2,2,2,128,256]{4,3,2,1,0:T(8,128)(2,1)} collective-permute-done((bf16[2,2,2,128,256]{4,3,2,1,0:T(8,128)(2,1)S(1)}, bf16[2,2,2,128,256]{4,3,2,1,0:T(8,128)(2,1)}, u32[]{:S(2)}, u32[]{:S(2)}) %collective-permute-start.12) | collective-permute-done | bytes 524320 | tf_op jit(solution)/shard_map/ppermute | solution.py:18
  289.5 4.7 %collective-permute-done.13 = bf16[2,2,128,256]{3,2,1,0:T(8,128)(2,1)S(1)} collective-permute-done((bf16[2,2,128,256]{3,2,1,0:T(8,128)(2,1)S(1)}, bf16[2,2,128,256]{3,2,1,0:T(8,128)(2,1)S(1)}, u32[]{:S(2)}, u32[]{:S(2)}) %collective-permute-start.13) | collective-permute-done | bytes 262176 | tf_op jit(solution)/shard_map/ppermute | solution.py:18
  297.5 6.8 %collective-permute-done.14 = bf16[2,128,256]{2,1,0:T(8,128)(2,1)S(1)} collective-permute-done((bf16[2,128,256]{2,1,0:T(8,128)(2,1)S(1)}, bf16[2,128,256]{2,1,0:T(8,128)(2,1)S(1)}, u32[]{:S(2)}, u32[]{:S(2)}) %collective-permute-start.14) | collective-permute-done | bytes 131104 | tf_op jit(solution)/shard_map/ppermute | solution.py:18
  307.0 3.2 %collective-permute-done.15 = f32[128,256]{0,1:T(8,128)S(1)} collective-permute-done((f32[128,256]{0,1:T(8,128)S(1)}, f32[128,256]{0,1:T(8,128)S(1)}, u32[]{:S(2)}, u32[]{:S(2)}) %collective-permute-start.15) | collective-permute-done | bytes 131104 | tf_op jit(solution)/shard_map/ppermute | solution.py:18
  310.2 2.1 collective-permute-done.27
  (150 shorter events, 61.1 us)
Async XLA Ops:
  1.3 15.0 %collective-permute-start = (bf16[64,4096]{1,0:T(8,128)(2,1)S(1)}, bf16[64,4096]{1,0:T(8,128)(2,1)S(1)}, u32[]{:S(2)}, u32[]{:S(2)}) collective-permute-start(bf16[64,4096]{1,0:T(8,128)(2,1)S(1)} %get-tuple-element.34), channel_id=1, source_target_pairs={{0,8},{8,0},{16,24},{24,16},{1,9},{9,1},{17,25},{25,17},{2,10},{10... | collective-permute-start | bytes 1572872 | tf_op jit(solution)/shard_map/ppermute | solution.py:18
  4.3 13.4 %collective-permute-start.2 = (bf16[64,4096]{1,0:T(8,128)(2,1)S(1)}, bf16[64,4096]{1,0:T(8,128)(2,1)S(1)}, u32[]{:S(2)}, u32[]{:S(2)}) collective-permute-start(bf16[64,4096]{1,0:T(8,128)(2,1)S(1)} %get-tuple-element.33), channel_id=1, source_target_pairs={{0,16},{8,24},{16,0},{24,8},{1,17},{9,25},{17,1},{25,9},{2,18},{10... | collective-permute-start | bytes 1572872 | tf_op jit(solution)/shard_map/ppermute | solution.py:18
  20.1 24.0 %collective-permute-start.1 = (bf16[2,64,4096]{2,1,0:T(8,128)(2,1)}, bf16[2,64,4096]{2,1,0:T(8,128)(2,1)S(1)}, u32[]{:S(2)}, u32[]{:S(2)}) collective-permute-start(bf16[2,64,4096]{2,1,0:T(8,128)(2,1)} %pad_maximum_fusion.1), channel_id=1, source_target_pairs={{0,16},{8,24},{16,0},{24,8},{1,17},{9,25},{17,1},{25,9},{2,18},{10... | collective-permute-start | bytes 3145736 | tf_op jit(solution)/shard_map/ppermute | solution.py:18
  22.7 23.8 %collective-permute-start.3 = (bf16[2,64,4096]{2,1,0:T(8,128)(2,1)}, bf16[2,64,4096]{2,1,0:T(8,128)(2,1)}, u32[]{:S(2)}, u32[]{:S(2)}) collective-permute-start(bf16[2,64,4096]{2,1,0:T(8,128)(2,1)} %pad_maximum_fusion.2), channel_id=1, source_target_pairs={{0,8},{8,0},{16,24},{24,16},{1,9},{9,1},{17,25},{25,17},{2,10},{10... | collective-permute-start | bytes 3145736 | tf_op jit(solution)/shard_map/ppermute | solution.py:18
  76.8 25.7 %collective-permute-start.4 = (bf16[4,1024,256]{2,1,0:T(8,128)(2,1)}, bf16[4,1024,256]{2,1,0:T(8,128)(2,1)}, u32[]{:S(2)}, u32[]{:S(2)}) collective-permute-start(bf16[4,1024,256]{2,1,0:T(8,128)(2,1)} %bitcast.19), channel_id=1, source_target_pairs={{0,1},{1,0},{2,3},{3,2},{4,5},{5,4},{6,7},{7,6},{8,9},{9,8},{10,11... | collective-permute-start | bytes 6291464 | tf_op jit(solution)/shard_map/ppermute | solution.py:18
  77.4 51.3 %collective-permute-start.16 = (bf16[4,1024,256]{2,1,0:T(8,128)(2,1)}, bf16[4,1024,256]{2,1,0:T(8,128)(2,1)S(1)}, u32[]{:S(2)}, u32[]{:S(2)}) collective-permute-start(bf16[4,1024,256]{2,1,0:T(8,128)(2,1)} %bitcast.151), channel_id=1, source_target_pairs={{0,1},{1,0},{2,3},{3,2},{4,5},{5,4},{6,7},{7,6},{8,9},{9,8},{10,11... | collective-permute-start | bytes 6291464 | tf_op jit(solution)/shard_map/ppermute | solution.py:18
  105.8 35.2 %copy-start.5 = (f32[4,1024,256]{2,1,0:T(8,128)}, f32[4,1024,256]{2,1,0:T(8,128)S(1)}, u32[]{:S(2)}) copy-start(f32[4,1024,256]{2,1,0:T(8,128)S(1)} %convert_add_fusion.1) | copy-start | bytes 12582916
  105.9 21.3 %collective-permute-start.5 = (bf16[1024,256]{1,0:T(8,128)(2,1)S(1)}, bf16[1024,256]{1,0:T(8,128)(2,1)S(1)}, u32[]{:S(2)}, u32[]{:S(2)}) collective-permute-start(bf16[1024,256]{1,0:T(8,128)(2,1)S(1)} %get-tuple-element.17), channel_id=1, source_target_pairs={{0,2},{1,3},{8,10},{9,11},{16,18},{17,19},{24,26},{25,27}} | collective-permute-start | bytes 1572872 | tf_op jit(solution)/shard_map/ppermute | solution.py:106
  126.5 9.3 %collective-permute-start.8 = (bf16[1024,256]{1,0:T(8,128)(2,1)S(1)}, bf16[1024,256]{1,0:T(8,128)(2,1)S(1)}, u32[]{:S(2)}, u32[]{:S(2)}) collective-permute-start(bf16[1024,256]{1,0:T(8,128)(2,1)S(1)} %get-tuple-element.18), channel_id=1, source_target_pairs={{6,4},{7,5},{14,12},{15,13},{22,20},{23,21},{30,28},{31,29}} | collective-permute-start | bytes 1572872 | tf_op jit(solution)/shard_map/ppermute | solution.py:107
  127.4 13.6 %collective-permute-start.6 = (bf16[1024,256]{1,0:T(8,128)(2,1)S(1)}, bf16[1024,256]{1,0:T(8,128)(2,1)S(1)}, u32[]{:S(2)}, u32[]{:S(2)}) collective-permute-start(bf16[1024,256]{1,0:T(8,128)(2,1)S(1)} %fusion.77), channel_id=1, source_target_pairs={{0,2},{1,3},{2,4},{3,5},{8,10},{9,11},{10,12},{11,13},{16,18},{17,... | collective-permute-start | bytes 1572872 | tf_op jit(solution)/shard_map/ppermute | solution.py:106
  132.4 19.0 %collective-permute-start.17 = (bf16[1024,256]{1,0:T(8,128)(2,1)}, bf16[1024,256]{1,0:T(8,128)(2,1)S(1)}, u32[]{:S(2)}, u32[]{:S(2)}) collective-permute-start(bf16[1024,256]{1,0:T(8,128)(2,1)} %get-tuple-element.21), channel_id=1, source_target_pairs={{0,2},{1,3},{8,10},{9,11},{16,18},{17,19},{24,26},{25,27}} | collective-permute-start | bytes 1572872 | tf_op jit(solution)/shard_map/ppermute | solution.py:106
  141.3 18.6 %collective-permute-start.9 = (bf16[1024,256]{1,0:T(8,128)(2,1)S(1)}, bf16[1024,256]{1,0:T(8,128)(2,1)}, u32[]{:S(2)}, u32[]{:S(2)}) collective-permute-start(bf16[1024,256]{1,0:T(8,128)(2,1)S(1)} %get-tuple-element.16), channel_id=1, source_target_pairs={{4,2},{5,3},{6,4},{7,5},{12,10},{13,11},{14,12},{15,13},{20,18},{2... | collective-permute-start | bytes 1572872 | tf_op jit(solution)/shard_map/ppermute | solution.py:107
  143.0 36.1 %copy-start.17 = (f32[1024]{0:T(1024)S(1)}, f32[1024]{0:T(1024)}, u32[]{:S(2)}) copy-start(f32[1024]{0:T(1024)} %param.11) | copy-start | bytes 12292
  143.0 20.5 %collective-permute-start.20 = (bf16[1024,256]{1,0:T(8,128)(2,1)}, bf16[1024,256]{1,0:T(8,128)(2,1)S(1)}, u32[]{:S(2)}, u32[]{:S(2)}) collective-permute-start(bf16[1024,256]{1,0:T(8,128)(2,1)} %get-tuple-element.22), channel_id=1, source_target_pairs={{6,4},{7,5},{14,12},{15,13},{22,20},{23,21},{30,28},{31,29}} | collective-permute-start | bytes 1572872 | tf_op jit(solution)/shard_map/ppermute | solution.py:107
  152.8 16.8 %collective-permute-start.18 = (bf16[1024,256]{1,0:T(8,128)(2,1)S(1)}, bf16[1024,256]{1,0:T(8,128)(2,1)S(1)}, u32[]{:S(2)}, u32[]{:S(2)}) collective-permute-start(bf16[1024,256]{1,0:T(8,128)(2,1)S(1)} %fusion.70), channel_id=1, source_target_pairs={{0,2},{1,3},{2,4},{3,5},{8,10},{9,11},{10,12},{11,13},{16,18},{17,... | collective-permute-start | bytes 1572872 | tf_op jit(solution)/shard_map/ppermute | solution.py:106
  157.3 21.8 %collective-permute-start.7 = (bf16[1024,256]{1,0:T(8,128)(2,1)S(1)}, bf16[1024,256]{1,0:T(8,128)(2,1)}, u32[]{:S(2)}, u32[]{:S(2)}) collective-permute-start(bf16[1024,256]{1,0:T(8,128)(2,1)S(1)} %get-tuple-element.15), channel_id=1, source_target_pairs={{0,2},{1,3},{2,4},{3,5},{4,6},{5,7},{8,10},{9,11},{10,12},{11,13},... | collective-permute-start | bytes 1572872 | tf_op jit(solution)/shard_map/ppermute | solution.py:106
  161.5 17.6 %collective-permute-start.10 = (bf16[1024,256]{1,0:T(8,128)(2,1)S(1)}, bf16[1024,256]{1,0:T(8,128)(2,1)}, u32[]{:S(2)}, u32[]{:S(2)}) collective-permute-start(bf16[1024,256]{1,0:T(8,128)(2,1)S(1)} %fusion.76), channel_id=1, source_target_pairs={{2,0},{3,1},{4,2},{5,3},{6,4},{7,5},{10,8},{11,9},{12,10},{13,11},... | collective-permute-start | bytes 1572872 | tf_op jit(solution)/shard_map/ppermute | solution.py:107
  171.3 31.9 %collective-permute-start.21 = (bf16[1024,256]{1,0:T(8,128)(2,1)S(1)}, bf16[1024,256]{1,0:T(8,128)(2,1)S(1)}, u32[]{:S(2)}, u32[]{:S(2)}) collective-permute-start(bf16[1024,256]{1,0:T(8,128)(2,1)S(1)} %get-tuple-element.20), channel_id=1, source_target_pairs={{4,2},{5,3},{6,4},{7,5},{12,10},{13,11},{14,12},{15,13},{20,18},{2... | collective-permute-start | bytes 1572872 | tf_op jit(solution)/shard_map/ppermute | solution.py:107
  183.3 41.8 %all-to-all-start = ((bf16[32,64,256]{2,1,0:T(8,128)(2,1)}), bf16[32,64,256]{2,1,0:T(8,128)(2,1)S(1)}, u32[]{:S(2)}, u32[]{:S(2)}) async-start(bf16[32,64,256]{2,1,0:T(8,128)(2,1)} %bitcast.27), calls=%async_computation | async-start | bytes 2097152 | tf_op jit(solution)/shard_map/all_to_all | solution.py:235
  199.5 17.1 %collective-permute-start.19 = (bf16[1024,256]{1,0:T(8,128)(2,1)S(1)}, bf16[1024,256]{1,0:T(8,128)(2,1)S(1)}, u32[]{:S(2)}, u32[]{:S(2)}) collective-permute-start(bf16[1024,256]{1,0:T(8,128)(2,1)S(1)} %get-tuple-element.19), channel_id=1, source_target_pairs={{0,2},{1,3},{2,4},{3,5},{4,6},{5,7},{8,10},{9,11},{10,12},{11,13},... | collective-permute-start | bytes 1572872 | tf_op jit(solution)/shard_map/ppermute | solution.py:106
  203.4 19.0 %collective-permute-start.22 = (bf16[1024,256]{1,0:T(8,128)(2,1)S(1)}, bf16[1024,256]{1,0:T(8,128)(2,1)S(1)}, u32[]{:S(2)}, u32[]{:S(2)}) collective-permute-start(bf16[1024,256]{1,0:T(8,128)(2,1)S(1)} %fusion.69), channel_id=1, source_target_pairs={{2,0},{3,1},{4,2},{5,3},{6,4},{7,5},{10,8},{11,9},{12,10},{13,11},... | collective-permute-start | bytes 1572872 | tf_op jit(solution)/shard_map/ppermute | solution.py:107
  225.1 33.1 %all-to-all-start.1 = ((bf16[32,64,256]{2,1,0:T(8,128)(2,1)}), bf16[32,64,256]{2,1,0:T(8,128)(2,1)S(1)}, u32[]{:S(2)}, u32[]{:S(2)}) async-start(bf16[32,64,256]{2,1,0:T(8,128)(2,1)} %bitcast.54), calls=%async_computation.1 | async-start | bytes 2097152 | tf_op jit(solution)/shard_map/all_to_all | solution.py:235
  241.1 27.2 %collective-permute-start.11 = (bf16[2,2,2,2,128,256]{5,4,3,2,1,0:T(8,128)(2,1)S(1)}, bf16[2,2,2,2,128,256]{5,4,3,2,1,0:T(8,128)(2,1)S(1)}, u32[]{:S(2)}, u32[]{:S(2)}) collective-permute-start(bf16[2,2,2,2,128,256]{5,4,3,2,1,0:T(8,128)(2,1)S(1)} %fusion.66), channel_id=1, source_target_pairs={{0,1},{1,0},{2,3},{3,2},{4,5},{5,4},{6,7},{7,6},{8,9},{9,8},{10,11... | collective-permute-start | bytes 3145736 | tf_op jit(solution)/shard_map/ppermute | solution.py:18
  268.2 3.2 %collective-permute-start.23 = (bf16[2,2,2,2,128,256]{5,4,3,2,1,0:T(8,128)(2,1)S(1)}, bf16[2,2,2,2,128,256]{5,4,3,2,1,0:T(8,128)(2,1)}, u32[]{:S(2)}, u32[]{:S(2)}) collective-permute-start(bf16[2,2,2,2,128,256]{5,4,3,2,1,0:T(8,128)(2,1)S(1)} %fusion.67), channel_id=1, source_target_pairs={{0,1},{1,0},{2,3},{3,2},{4,5},{5,4},{6,7},{7,6},{8,9},{9,8},{10,11... | collective-permute-start | bytes 3145736 | tf_op jit(solution)/shard_map/ppermute | solution.py:18
  270.4 14.4 %collective-permute-start.12 = (bf16[2,2,2,128,256]{4,3,2,1,0:T(8,128)(2,1)S(1)}, bf16[2,2,2,128,256]{4,3,2,1,0:T(8,128)(2,1)}, u32[]{:S(2)}, u32[]{:S(2)}) collective-permute-start(bf16[2,2,2,128,256]{4,3,2,1,0:T(8,128)(2,1)S(1)} %fusion.86), channel_id=1, source_target_pairs={{0,8},{8,0},{16,24},{24,16},{1,9},{9,1},{17,25},{25,17},{2,10},{10... | collective-permute-start | bytes 1572872 | tf_op jit(solution)/shard_map/ppermute | solution.py:18
  273.0 14.2 %collective-permute-start.24 = (bf16[2,2,2,128,256]{4,3,2,1,0:T(8,128)(2,1)S(1)}, bf16[2,2,2,128,256]{4,3,2,1,0:T(8,128)(2,1)}, u32[]{:S(2)}, u32[]{:S(2)}) collective-permute-start(bf16[2,2,2,128,256]{4,3,2,1,0:T(8,128)(2,1)S(1)} %fusion.89), channel_id=1, source_target_pairs={{0,16},{8,24},{16,0},{24,8},{1,17},{9,25},{17,1},{25,9},{2,18},{10... | collective-permute-start | bytes 1572872 | tf_op jit(solution)/shard_map/ppermute | solution.py:18
  286.4 7.9 %collective-permute-start.13 = (bf16[2,2,128,256]{3,2,1,0:T(8,128)(2,1)S(1)}, bf16[2,2,128,256]{3,2,1,0:T(8,128)(2,1)S(1)}, u32[]{:S(2)}, u32[]{:S(2)}) collective-permute-start(bf16[2,2,128,256]{3,2,1,0:T(8,128)(2,1)S(1)} %fusion.95), channel_id=1, source_target_pairs={{0,16},{8,24},{16,0},{24,8},{1,17},{9,25},{17,1},{25,9},{2,18},{10... | collective-permute-start | bytes 786440 | tf_op jit(solution)/shard_map/ppermute | solution.py:18
  288.4 7.6 %collective-permute-start.25 = (bf16[2,2,128,256]{3,2,1,0:T(8,128)(2,1)S(1)}, bf16[2,2,128,256]{3,2,1,0:T(8,128)(2,1)S(1)}, u32[]{:S(2)}, u32[]{:S(2)}) collective-permute-start(bf16[2,2,128,256]{3,2,1,0:T(8,128)(2,1)S(1)} %fusion.96), channel_id=1, source_target_pairs={{0,8},{8,0},{16,24},{24,16},{1,9},{9,1},{17,25},{25,17},{2,10},{10... | collective-permute-start | bytes 786440 | tf_op jit(solution)/shard_map/ppermute | solution.py:18
  294.3 10.0 %collective-permute-start.14 = (bf16[2,128,256]{2,1,0:T(8,128)(2,1)S(1)}, bf16[2,128,256]{2,1,0:T(8,128)(2,1)S(1)}, u32[]{:S(2)}, u32[]{:S(2)}) collective-permute-start(bf16[2,128,256]{2,1,0:T(8,128)(2,1)S(1)} %fusion.98), channel_id=1, source_target_pairs={{0,4},{1,5},{2,6},{3,7},{4,0},{5,1},{6,2},{7,3},{8,12},{9,13},{10,... | collective-permute-start | bytes 393224 | tf_op jit(solution)/shard_map/ppermute | solution.py:18
  296.1 10.4 %collective-permute-start.26 = (bf16[2,128,256]{2,1,0:T(8,128)(2,1)S(1)}, bf16[2,128,256]{2,1,0:T(8,128)(2,1)S(1)}, u32[]{:S(2)}, u32[]{:S(2)}) collective-permute-start(bf16[2,128,256]{2,1,0:T(8,128)(2,1)S(1)} %fusion.99), channel_id=1, source_target_pairs={{0,4},{1,5},{2,6},{3,7},{4,0},{5,1},{6,2},{7,3},{8,12},{9,13},{10,... | collective-permute-start | bytes 393224 | tf_op jit(solution)/shard_map/ppermute | solution.py:18
  304.5 5.7 %collective-permute-start.15 = (f32[128,256]{0,1:T(8,128)S(1)}, f32[128,256]{0,1:T(8,128)S(1)}, u32[]{:S(2)}, u32[]{:S(2)}) collective-permute-start(f32[128,256]{0,1:T(8,128)S(1)} %bitcast.167), channel_id=1, source_target_pairs={{0,2},{1,3},{2,0},{3,1},{4,6},{5,7},{6,4},{7,5},{8,10},{9,11},{10,... | collective-permute-start | bytes 393224 | tf_op jit(solution)/shard_map/ppermute | solution.py:18
  306.8 5.5 %collective-permute-start.27 = (f32[128,256]{0,1:T(8,128)S(1)}, f32[128,256]{0,1:T(8,128)S(1)}, u32[]{:S(2)}, u32[]{:S(2)}) collective-permute-start(f32[128,256]{0,1:T(8,128)S(1)} %bitcast.168), channel_id=1, source_target_pairs={{0,2},{1,3},{2,0},{3,1},{4,6},{5,7},{6,4},{7,5},{8,10},{9,11},{10,... | collective-permute-start | bytes 393224 | tf_op jit(solution)/shard_map/ppermute | solution.py:18
  (16 other events, 209.7 us)

commit v2 on v1

--- a/solution.py
+++ b/solution.py
@@ -31,9 +31,11 @@
         low = (me // bit) % 2 == 0
         held = jnp.stack([jnp.where(low, held, other), jnp.where(low, other, held)], axis=0)
         axes.insert(0, bit)
+        if len(axes) == 1:
+            held = yield held
     rank = [axes.index(bit) for bit in sorted(axes, reverse=True)]
     held = held.transpose(tuple(rank) + (len(axes), len(axes) + 1))
-    return held.reshape(-1, block.shape[1])
+    yield held.reshape(-1, block.shape[1])
 
 
 def panel_kernel(side_ref, factor_ref, *refs):
@@ -47,27 +49,29 @@
         ).astype(out_ref.dtype)
 
 
-def half_field(chol_factor, panels, side, line, block, dtype):
+def send_order(line):
+    return [sorted(range(line), key=lambda b: (-abs(b - p), -b)) for p in range(line)]
+
+
+def block_field(chol_factor, panels, blocks, block, dtype):
     depth = chol_factor.shape[1]
     tile = min(512, block)
     per_block = block // tile
-    panel_specs = [pl.BlockSpec(p.shape, lambda i, j, side: (0, 0)) for p in panels]
+    panel_specs = [pl.BlockSpec(p.shape, lambda i, j, which: (0, 0)) for p in panels]
     out_specs = [
-        pl.BlockSpec((tile, p.shape[0]), lambda i, j, side: (i * per_block + j, 0))
+        pl.BlockSpec((tile, p.shape[0]), lambda i, j, which: (i * per_block + j, 0))
         for p in panels
     ]
-    rows = line * block
+    count = blocks.shape[0]
+    rows = count * block
     events = sum(p.shape[0] for p in panels)
-    return pl.pallas_call(
+    outs = pl.pallas_call(
         panel_kernel,
         grid_spec=pltpu.PrefetchScalarGridSpec(
             num_scalar_prefetch=1,
-            grid=(line, per_block),
+            grid=(count, per_block),
             in_specs=[
-                pl.BlockSpec(
-                    (tile, depth),
-                    lambda i, j, side: ((2 * i + side[0]) * per_block + j, 0),
-                )
+                pl.BlockSpec((tile, depth), lambda i, j, which: (which[i] * per_block + j, 0))
             ]
             + panel_specs,
             out_specs=out_specs,
@@ -79,33 +83,53 @@
             bytes_accessed=2 * rows * depth + 4 * rows * events,
             transcendentals=0,
         ),
-    )(side.reshape(1).astype(jnp.int32), chol_factor, *panels)
+    )(blocks.astype(jnp.int32), chol_factor, *panels)
+    return [o.reshape(count, block, o.shape[1]) for o in outs]
 
 
 def field_scatter(mine, theirs):
     me = lax.axis_index("col")
-    line = mine.shape[0]
+    line = sum(m.shape[0] for m in mine)
+    first = mine[0].shape[0]
     place = me // 2
-    summed = mine + swap(theirs, "col", 1).astype(jnp.float32)
+    order = send_order(line)
+    where = [[order[p].index(b) for b in range(line)] for p in range(line)]
+    summed = [m + swap(t, "col", 1).astype(jnp.float32) for m, t in zip(mine, theirs)]
+
+    def take(wanted):
+        spots = [where[p][b] if b is not None else 0 for p, b in enumerate(wanted)]
+        spot = sum(jnp.where(place == p, k, 0) for p, k in enumerate(spots))
+        early = lax.dynamic_index_in_dim(
+            summed[0], jnp.minimum(spot, first - 1), 0, keepdims=False
+        )
+        if max(spots) < first:
+            return early
+        late = lax.dynamic_index_in_dim(
+            summed[1], jnp.maximum(spot - first, 0), 0, keepdims=False
+        )
+        if min(spots) >= first:
+            return late
+        return jnp.where(spot < first, early, late)
+
     up = down = None
     for step in range(1, line):
-        index_up = jnp.clip(place + line - step, 0, line - 1)
-        index_down = jnp.clip(place - line + step, 0, line - 1)
-        send_up = lax.dynamic_index_in_dim(summed, index_up, 0, keepdims=False)
-        send_down = lax.dynamic_index_in_dim(summed, index_down, 0, keepdims=False)
+        reach = line - step
+        blocks_up = [p + reach if p + reach < line else None for p in range(line)]
+        blocks_down = [p - reach if p - reach >= 0 else None for p in range(line)]
+        send_up, send_down = take(blocks_up), take(blocks_down)
         if up is not None:
             send_up = send_up + up.astype(jnp.float32)
             send_down = send_down + down.astype(jnp.float32)
         pairs_up, pairs_down = [], []
         for p in range(line):
             for c in range(2):
-                if p < step and p + 1 < line:
+                if blocks_up[p] is not None:
                     pairs_up.append((2 * p + c, 2 * p + 2 + c))
-                if p >= line - step and p > 0:
+                if blocks_down[p] is not None:
                     pairs_down.append((2 * p + c, 2 * p - 2 + c))
         up = lax.ppermute(send_up.astype(jnp.bfloat16), "col", pairs_up)
         down = lax.ppermute(send_down.astype(jnp.bfloat16), "col", pairs_down)
-    own = lax.dynamic_index_in_dim(summed, place, 0, keepdims=False)
+    own = take(list(range(line)))
     if up is not None:
         own = own + up.astype(jnp.float32) + down.astype(jnp.float32)
     return own
@@ -125,10 +149,12 @@
         side = (lax.axis_index(axis) // bit) % 2
         give = lax.dynamic_index_in_dim(held, 1 - side, where, keepdims=False)
         keep = lax.dynamic_index_in_dim(held, side, where, keepdims=False)
-        if number < len(steps) - 1:
+        if number < len(steps) - 2:
             give = give.astype(jnp.bfloat16)
         held = keep + swap(give, axis, bit).astype(jnp.float32)
-    return held
+        if number == 1:
+            held = yield held
+    yield held
 
 
 def split3(value):
@@ -160,6 +186,10 @@
     for chunk in range(CHUNKS):
         order = row_bits if chunk % 2 == 0 else row_bits[::-1]
         gathered.append(gather_rows(normals[chunk * part : (chunk + 1) * part], order))
+    starts, asset_zone, site_region = lax.optimization_barrier(
+        ([next(g) for g in gathered], asset_zone, site_region)
+    )
+    gathered = [g.send(start) for g, start in zip(gathered, starts)]
 
     site_count = site_median.shape[0]
     slot_cap = max(2, 2 * site_count // device_count)
@@ -209,6 +239,9 @@
         jnp.bfloat16
     )
     placed = jnp.dot(order_of, table, preferred_element_type=jnp.float32)
+    gathered, slot_rank, placed, selector = lax.optimization_barrier(
+        (gathered, slot_rank, placed, selector)
+    )
     capacity = placed[:, 0] + placed[:, 1] + placed[:, 2]
     beta = placed[:, 3] + placed[:, 4] + placed[:, 5]
     value = placed[:, 6] + placed[:, 7] + placed[:, 8]
@@ -219,14 +252,28 @@
     ).astype(jnp.bfloat16)
     chooser = (pick[:, None] == slot_rank[None, :]).astype(jnp.bfloat16)
 
-    line, core = cols // 2, lax.axis_index("col") % 2
-    theirs = half_field(chol_factor, gathered, 1 - core, line, site_count, jnp.bfloat16)
-    mine = half_field(chol_factor, gathered, core, line, site_count, jnp.float32)
-
+    line, me = cols // 2, lax.axis_index("col")
+    core = me % 2
+    table_of = jnp.asarray(send_order(line), jnp.int32)
+    blocks = lax.dynamic_index_in_dim(table_of, me // 2, 0, keepdims=False)
+    first = (line + 1) // 2
+    theirs, mine = [], []
+    for half in (blocks[:first], blocks[first:]):
+        if half.shape[0] > 0:
+            theirs.append(
+                block_field(chol_factor, gathered, 2 * half + 1 - core, site_count, jnp.bfloat16)
+            )
+            mine.append(
+                block_field(chol_factor, gathered, 2 * half + core, site_count, jnp.float32)
+            )
+
+    fields = [
+        field_scatter([m[chunk] for m in mine], [t[chunk] for t in theirs])
+        for chunk in range(CHUNKS)
+    ]
     results = []
     for chunk in range(CHUNKS):
-        shape = (line, site_count, rows * part)
-        field = field_scatter(mine[chunk].reshape(shape), theirs[chunk].reshape(shape))
+        field = fields[chunk]
         log_motion = (site_median[:, None] + field).astype(jnp.bfloat16)
         events = log_motion.shape[1]
         outgoing = jnp.dot(selector, log_motion, preferred_element_type=jnp.float32).astype(
@@ -250,7 +297,11 @@
             preferred_element_type=jnp.float32,
         )
         order = row_bits if chunk % 2 == 0 else row_bits[::-1]
-        zones = zone_scatter(zone_table, order)
+        steps = zone_scatter(zone_table, order)
+        zones = next(steps)
+        if chunk + 1 < CHUNKS:
+            zones, fields[chunk + 1] = lax.optimization_barrier((zones, fields[chunk + 1]))
+        zones = steps.send(zones)
         results.append(zones.reshape(zone_share, rows, part))
     return jnp.stack(results, axis=2).reshape(zone_share, rows * local_events)
 

time: 314 us -> 346 us (1.10)
  blocking collectives: 0 us -> 32.4 us
  waiting for transfers between devices: 123 us -> 107 us
  local copies, waits for them, and re-layouts: 15.6 us -> 23.2 us
  Pallas kernels: 47.2 us -> 53.4 us
    all_to_all x0 -> x1, blocking collectives: none -> 32.4 us  [per_device(): lax.all_to_all(outgoing.reshape(device_count, slot_cap, events), ('row',...]
    ppermute x6, waiting for transfers between devices: 37.8 us -> 13.6 us  [field_scatter(): up = lax.ppermute(send_up.astype(jnp.bfloat16), 'col', pairs_up)]
    ppermute x6, waiting for transfers between devices: 5.77 us -> 14.1 us  [field_scatter(): down = lax.ppermute(send_down.astype(jnp.bfloat16), 'col', pairs_down)]
    pallas_call x2 -> x4, Pallas kernels: 47.2 us -> 53.4 us  [block_field(): pl.pallas_call(panel_kernel, grid_spec=pltpu.PrefetchScalarGridSpec(num_s...]
    ppermute x6, starting transfers between devices: 19.2 us -> 24.1 us  [field_scatter(): up = lax.ppermute(send_up.astype(jnp.bfloat16), 'col', pairs_up)]
    another operation x5, other arithmetic: 6.5 us -> 2.03 us  [gather_rows(): jnp.stack([jnp.where(low, held, other), jnp.where(low, other, held)], axi...]
    another operation x13, local copies, waits for them, and re-layouts: 0.43 us -> 4.84 us  [per_device(): jnp.stack(split3(asset_capacity) + split3(asset_beta) + split3(asset_valu...]
    all_to_all x2 -> x1, starting transfers between devices: 10.3 us -> 6 us  [per_device(): lax.all_to_all(outgoing.reshape(device_count, slot_cap, events), ('row',...]
  transfers between devices with their start and end apart: 30 -> 31, of which waited for: 19 -> 20; matrix products, arithmetic and copies ran while one was open for 24% -> 13% of each run, Pallas kernels for 7% -> 12%
where the time goes in v2:
time: 346 us; the launch traced here: 345 us
  waiting for transfers between devices  107 us (31%)
  matrix products  53.7 us (16%)
  Pallas kernels  53.4 us (15%)
  starting transfers between devices  47.7 us (14%)
  blocking collectives  32.4 us (9%)
  other arithmetic  25 us (7%)
  local copies, waits for them, and re-layouts  23.2 us (7%)
    ppermute x18, waiting for transfers between devices, swap(): return lax.ppermute(value, axis, [(i, i ^ bit) for i in range(size)])  63.9 us
    pallas_call x4, Pallas kernels, block_field(): pl.pallas_call(panel_kernel, grid_spec=pltpu.PrefetchScalarGridSpec(num_s...  53.4 us
    all_to_all x1, blocking collectives, per_device(): lax.all_to_all(outgoing.reshape(device_count, slot_cap, events), ('row',...  32.4 us
    ppermute x6, starting transfers between devices, field_scatter(): up = lax.ppermute(send_up.astype(jnp.bfloat16), 'col', pairs_up)  24.1 us
    dot_general x2, matrix products, rank_of(): running = jnp.dot(before, onehot, preferred_element_type=jnp.float32)  17.6 us
    all_to_all x1, waiting for transfers between devices, per_device(): lax.all_to_all(outgoing.reshape(device_count, slot_cap, events), ('row',...  16 us
    dot_general x2, matrix products, per_device(): motion = jnp.dot(chooser, incoming, preferred_element_type=jnp.float32)  14.3 us
    ppermute x6, waiting for transfers between devices, field_scatter(): down = lax.ppermute(send_down.astype(jnp.bfloat16), 'col', pairs_down)  14.1 us
  transfers between devices with their start and end apart: 31, of which 20 were waited for; matrix products, arithmetic and copies ran while one was open for 13% of the time, Pallas kernels for 12%

profile of v2, /device:TPU:0, one launch (start us, length us, event | category | flops | bytes accessed | tf_op | source)
XLA Modules:
  0.0 345.0 jit_solution(9451504641850192246)
XLA Ops:
  1.4 3.0 collective-permute-start
  7.6 8.8 %collective-permute-done = bf16[64,4096]{1,0:T(8,128)(2,1)S(1)} collective-permute-done((bf16[64,4096]{1,0:T(8,128)(2,1)S(1)}, bf16[64,4096]{1,0:T(8,128)(2,1)S(1)}, u32[]{:S(2)}, u32[]{:S(2)}) %collective-permute-start) | collective-permute-done | bytes 524320 | tf_op jit(solution)/shard_map/ppermute | solution.py:18
  23.4 17.1 %fusion.58 = f32[4096]{0:T(1024)S(1)} fusion(s32[4096]{0:T(1024)S(1)} %add_select_fusion.4), kind=kOutput, calls=%fused_computation.47 | convolution fusion | flops 1091301376 | bytes 32768 | tf_op jit(solution)/shard_map/dot_general | solution.py:206
  47.7 4.1 %fusion.11 = bf16[2048,1024]{1,0:T(8,128)(2,1)} fusion(s32[1024]{0:T(1024)S(1)} %bitcast.186), kind=kLoop, calls=%fused_computation.14 | loop fusion | flops 4194304 | bytes 4198400 | tf_op jit(solution)/shard_map/convert_element_type | solution.py:210
  51.8 11.7 %fusion.1 = f32[4096,12]{0,1:T(8,128)S(1)} fusion(bf16[4096,12]{0,1:T(8,128)(2,1)S(1)} %copy-done.17, s32[4096]{0:T(1024)S(1)} %copy-done.19), kind=kOutput, calls=%fused_computation.3 | convolution fusion | flops 419430400 | bytes 311296 | tf_op jit(solution)/shard_map/dot_general | solution.py:241
  69.1 13.1 %shard_map.103 = (bf16[2048,256]{1,0:T(8,128)(2,1)S(1)}, bf16[2048,256]{1,0:T(8,128)(2,1)S(1)}) custom-call(s32[2]{0:T(128)S(1)} %get-tuple-element.85.side_ref, bf16[8192,4096]{1,0:T(8,128)(2,1)} %factor_ref.7, bf16[256,4096]{1,0:T(8,128)(2,1)S(1)} %bitcast.156, bf16[256,4096]{1,0:T(8,128)(2,1)} %bitcast.168), custom_call_target="tpu_custom_call" | custom-call | flops 8589934592 | bytes 20971520 | tf_op jit(solution)/shard_map/pallas_call | solution.py:68
  82.3 13.8 %shard_map.102 = (f32[2048,256]{1,0:T(8,128)S(1)}, f32[2048,256]{1,0:T(8,128)S(1)}) custom-call(s32[2]{0:T(128)S(1)} %get-tuple-element.84.side_ref, bf16[8192,4096]{1,0:T(8,128)(2,1)} %factor_ref.7, bf16[256,4096]{1,0:T(8,128)(2,1)} %bitcast.157, bf16[256,4096]{1,0:T(8,128)(2,1)} %bitcast.169), custom_call_target="tpu_custom_call" | custom-call | flops 8589934592 | bytes 20971520 | tf_op jit(solution)/shard_map/pallas_call | solution.py:68
  97.5 3.4 collective-permute-start.6
  101.7 13.0 %shard_map.101 = (bf16[2048,256]{1,0:T(8,128)(2,1)S(1)}, bf16[2048,256]{1,0:T(8,128)(2,1)S(1)}) custom-call(s32[2]{0:T(128)S(1)} %get-tuple-element.83.side_ref, bf16[8192,4096]{1,0:T(8,128)(2,1)} %factor_ref.7, bf16[256,4096]{1,0:T(8,128)(2,1)S(1)} %bitcast.159, bf16[256,4096]{1,0:T(8,128)(2,1)} %bitcast.170), custom_call_target="tpu_custom_call" | custom-call | flops 8589934592 | bytes 20971520 | tf_op jit(solution)/shard_map/pallas_call | solution.py:68
  118.7 13.6 %shard_map.100 = (f32[2048,256]{1,0:T(8,128)S(1)}, f32[2048,256]{1,0:T(8,128)S(1)}) custom-call(s32[2]{0:T(128)S(1)} %get-tuple-element.86.side_ref, bf16[8192,4096]{1,0:T(8,128)(2,1)} %factor_ref.7, bf16[256,4096]{1,0:T(8,128)(2,1)} %bitcast.158, bf16[256,4096]{1,0:T(8,128)(2,1)} %bitcast.171), custom_call_target="tpu_custom_call" | custom-call | flops 8589934592 | bytes 20971520 | tf_op jit(solution)/shard_map/pallas_call | solution.py:68
  135.5 6.3 %collective-permute-start.8 = (bf16[1024,256]{1,0:T(8,128)(2,1)}, bf16[1024,256]{1,0:T(8,128)(2,1)}, u32[]{:S(2)}, u32[]{:S(2)}) collective-permute-start(bf16[1024,256]{1,0:T(8,128)(2,1)} %get-tuple-element.47), channel_id=1, source_target_pairs={{0,2},{1,3},{2,4},{3,5},{4,6},{5,7},{8,10},{9,11},{10,12},{11,13},... | collective-permute-start | bytes 1572872 | tf_op jit(solution)/shard_map/ppermute | solution.py:130
  141.8 8.9 %collective-permute-done.11 = bf16[1024,256]{1,0:T(8,128)(2,1)} collective-permute-done((bf16[1024,256]{1,0:T(8,128)(2,1)}, bf16[1024,256]{1,0:T(8,128)(2,1)}, u32[]{:S(2)}, u32[]{:S(2)}) %collective-permute-start.11) | collective-permute-done | bytes 524320 | tf_op jit(solution)/shard_map/ppermute | solution.py:131
  151.9 5.1 %convolution_convert_fusion.1 = bf16[2048,256]{1,0:T(8,128)(2,1)} fusion(bf16[2048,1024]{1,0:T(8,128)(2,1)} %fusion.11, bf16[1024,256]{1,0:T(8,128)(2,1)} %collective-permute-done.11, bf16[1024,256]{1,0:T(8,128)(2,1)} %collective-permute-done.8, f32[2,1024,256]{2,1,0:T(8,128)} %copy-done.12, s32[]{:T(128)S(6)} %max.12, f32[1024]{0:T(1024)S(1)} %copy-done.25), kind=kOutput, calls=%fused_computation.33 | convolution fusion | flops 1075838976 | bytes 7344132 | tf_op jit(solution)/shard_map/dot_general | solution.py:279
  157.0 6.0 %all-to-all-start = ((bf16[32,64,256]{2,1,0:T(8,128)(2,1)}), bf16[32,64,256]{2,1,0:T(8,128)(2,1)}, u32[]{:S(2)}, u32[]{:S(2)}) async-start(bf16[32,64,256]{2,1,0:T(8,128)(2,1)} %bitcast.178), calls=%async_computation | async-start | bytes 2097152 | tf_op jit(solution)/shard_map/all_to_all | solution.py:282
  170.2 3.6 %collective-permute-start.16 = (bf16[1024,256]{1,0:T(8,128)(2,1)}, bf16[1024,256]{1,0:T(8,128)(2,1)S(1)}, u32[]{:S(2)}, u32[]{:S(2)}) collective-permute-start(bf16[1024,256]{1,0:T(8,128)(2,1)} %fusion.81), channel_id=1, source_target_pairs={{0,2},{1,3},{8,10},{9,11},{16,18},{17,19},{24,26},{25,27}} | collective-permute-start | bytes 1572872 | tf_op jit(solution)/shard_map/ppermute | solution.py:130
  174.5 16.0 %all-to-all-done = bf16[32,64,256]{2,1,0:T(8,128)(2,1)} async-done(((bf16[32,64,256]{2,1,0:T(8,128)(2,1)}), bf16[32,64,256]{2,1,0:T(8,128)(2,1)}, u32[]{:S(2)}, u32[]{:S(2)}) %all-to-all-start) | async-done | bytes 1048608 | tf_op jit(solution)/shard_map/all_to_all | solution.py:282
  190.5 7.2 %fusion.51 = bf16[4096,256]{1,0:T(8,128)(2,1)S(1)} fusion(bf16[2048,256]{1,0:T(8,128)(2,1)} %bitcast.31, s32[2048]{0:T(1024)S(1)} %copy-done.24, s32[4096]{0:T(1024)S(1)} %bitcast.191, f32[4096]{0:T(1024)S(1)} %bitcast.187, f32[4096]{0:T(1024)S(1)} %bitcast.189, f32[4096]{0:T(1024)S(1)} %bitcast.193), kind=kOutput, calls=%fused_computation.28 | convolution fusion | flops 4309647360 | bytes 3219456 | tf_op jit(solution)/shard_map/dot_general | solution.py:289
  206.6 9.2 %collective-permute-done.17 = bf16[1024,256]{1,0:T(8,128)(2,1)S(1)} collective-permute-done((bf16[1024,256]{1,0:T(8,128)(2,1)}, bf16[1024,256]{1,0:T(8,128)(2,1)S(1)}, u32[]{:S(2)}, u32[]{:S(2)}) %collective-permute-start.17) | collective-permute-done | bytes 524320 | tf_op jit(solution)/shard_map/ppermute | solution.py:130
  216.3 7.1 %collective-permute-start.18 = (bf16[1024,256]{1,0:T(8,128)(2,1)S(1)}, bf16[1024,256]{1,0:T(8,128)(2,1)}, u32[]{:S(2)}, u32[]{:S(2)}) collective-permute-start(bf16[1024,256]{1,0:T(8,128)(2,1)S(1)} %get-tuple-element.45), channel_id=1, source_target_pairs={{0,2},{1,3},{2,4},{3,5},{4,6},{5,7},{8,10},{9,11},{10,12},{11,13},... | collective-permute-start | bytes 1572872 | tf_op jit(solution)/shard_map/ppermute | solution.py:130
  230.1 3.1 collective-permute-done.18
  233.3 5.1 %collective-permute-done.21 = bf16[1024,256]{1,0:T(8,128)(2,1)} collective-permute-done((bf16[1024,256]{1,0:T(8,128)(2,1)S(1)}, bf16[1024,256]{1,0:T(8,128)(2,1)}, u32[]{:S(2)}, u32[]{:S(2)}) %collective-permute-start.21) | collective-permute-done | bytes 524320 | tf_op jit(solution)/shard_map/ppermute | solution.py:131
  242.9 3.6 %convolution_convert_fusion = bf16[2048,256]{1,0:T(8,128)(2,1)S(1)} fusion(bf16[2048,1024]{1,0:T(8,128)(2,1)} %fusion.11, f32[1024,256]{1,0:T(8,128)S(1)} %fusion.67, f32[1024]{0:T(1024)S(1)} %copy-done.25), kind=kOutput, calls=%fused_computation.32 | convolution fusion | flops 1074790400 | bytes 6295552 | tf_op jit(solution)/shard_map/dot_general | solution.py:279
  246.5 32.4 %all_to_all.10 = bf16[32,64,256]{2,1,0:T(8,128)(2,1)S(1)} all-to-all(bf16[32,64,256]{2,1,0:T(8,128)(2,1)S(1)} %bitcast.180), channel_id=1, replica_groups=mesh['row'=4,'col'=8] {'row','col'}, dimensions={0} | all-to-all | bytes 2097152 | tf_op jit(solution)/shard_map/all_to_all | solution.py:282
  278.9 7.2 %fusion.33 = bf16[4096,256]{1,0:T(8,128)(2,1)S(1)} fusion(bf16[2048,256]{1,0:T(8,128)(2,1)S(1)} %bitcast.179, s32[2048]{0:T(1024)S(1)} %copy-done.24, s32[4096]{0:T(1024)S(1)} %bitcast.192, f32[4096]{0:T(1024)S(1)} %bitcast.188, f32[4096]{0:T(1024)S(1)} %bitcast.190, f32[4096]{0:T(1024)S(1)} %bitcast.194), kind=kOutput, calls=%fused_computation.22 | convolution fusion | flops 4309647360 | bytes 3219456 | tf_op jit(solution)/shard_map/dot_general | solution.py:289
  289.0 2.8 collective-permute-done.25
  297.0 13.0 %collective-permute-done.26 = bf16[2,2,2,128,256]{4,3,2,1,0:T(8,128)(2,1)} collective-permute-done((bf16[2,2,2,128,256]{4,3,2,1,0:T(8,128)(2,1)}, bf16[2,2,2,128,256]{4,3,2,1,0:T(8,128)(2,1)}, u32[]{:S(2)}, u32[]{:S(2)}) %collective-permute-start.26) | collective-permute-done | bytes 524320 | tf_op jit(solution)/shard_map/ppermute | solution.py:18
  311.8 2.8 collective-permute-done.22
  314.8 3.1 collective-permute-done.27
  318.1 14.8 %collective-permute-done.23 = f32[2,128,256]{2,1,0:T(8,128)S(1)} collective-permute-done((f32[2,128,256]{2,1,0:T(8,128)S(1)}, f32[2,128,256]{2,1,0:T(8,128)S(1)}, u32[]{:S(2)}, u32[]{:S(2)}) %collective-permute-start.23) | collective-permute-done | bytes 262176 | tf_op jit(solution)/shard_map/ppermute | solution.py:18
  333.0 5.5 %collective-permute-done.28 = f32[2,128,256]{2,1,0:T(8,128)S(1)} collective-permute-done((f32[2,128,256]{2,1,0:T(8,128)S(1)}, f32[2,128,256]{2,1,0:T(8,128)S(1)}, u32[]{:S(2)}, u32[]{:S(2)}) %collective-permute-start.28) | collective-permute-done | bytes 262176 | tf_op jit(solution)/shard_map/ppermute | solution.py:18
  338.7 2.6 collective-permute-done.24
  341.4 2.7 collective-permute-done.29
  (173 shorter events, 73.2 us)
Async XLA Ops:
  1.4 15.0 %collective-permute-start = (bf16[64,4096]{1,0:T(8,128)(2,1)S(1)}, bf16[64,4096]{1,0:T(8,128)(2,1)S(1)}, u32[]{:S(2)}, u32[]{:S(2)}) collective-permute-start(bf16[64,4096]{1,0:T(8,128)(2,1)S(1)} %get-tuple-element.64), channel_id=1, source_target_pairs={{0,8},{8,0},{16,24},{24,16},{1,9},{9,1},{17,25},{25,17},{2,10},{10... | collective-permute-start | bytes 1572872 | tf_op jit(solution)/shard_map/ppermute | solution.py:18
  4.4 13.4 %collective-permute-start.1 = (bf16[64,4096]{1,0:T(8,128)(2,1)S(1)}, bf16[64,4096]{1,0:T(8,128)(2,1)S(1)}, u32[]{:S(2)}, u32[]{:S(2)}) collective-permute-start(bf16[64,4096]{1,0:T(8,128)(2,1)S(1)} %get-tuple-element.63), channel_id=1, source_target_pairs={{0,16},{8,24},{16,0},{24,8},{1,17},{9,25},{17,1},{25,9},{2,18},{10... | collective-permute-start | bytes 1572872 | tf_op jit(solution)/shard_map/ppermute | solution.py:18
  41.7 23.8 %collective-permute-start.3 = (bf16[2,64,4096]{2,1,0:T(8,128)(2,1)S(1)}, bf16[2,64,4096]{2,1,0:T(8,128)(2,1)S(1)}, u32[]{:S(2)}, u32[]{:S(2)}) collective-permute-start(bf16[2,64,4096]{2,1,0:T(8,128)(2,1)S(1)} %get-tuple-element.25), channel_id=1, source_target_pairs={{0,8},{8,0},{16,24},{24,16},{1,9},{9,1},{17,25},{25,17},{2,10},{10... | collective-permute-start | bytes 3145736 | tf_op jit(solution)/shard_map/ppermute | solution.py:18
  43.7 23.9 %collective-permute-start.2 = (bf16[2,64,4096]{2,1,0:T(8,128)(2,1)S(1)}, bf16[2,64,4096]{2,1,0:T(8,128)(2,1)}, u32[]{:S(2)}, u32[]{:S(2)}) collective-permute-start(bf16[2,64,4096]{2,1,0:T(8,128)(2,1)S(1)} %get-tuple-element.24), channel_id=1, source_target_pairs={{0,16},{8,24},{16,0},{24,8},{1,17},{9,25},{17,1},{25,9},{2,18},{10... | collective-permute-start | bytes 3145736 | tf_op jit(solution)/shard_map/ppermute | solution.py:18
  82.2 13.9 %collective-permute-start.5 = (bf16[2,1024,256]{2,1,0:T(8,128)(2,1)S(1)}, bf16[2,1024,256]{2,1,0:T(8,128)(2,1)S(1)}, u32[]{:S(2)}, u32[]{:S(2)}) collective-permute-start(bf16[2,1024,256]{2,1,0:T(8,128)(2,1)S(1)} %bitcast.166), channel_id=1, source_target_pairs={{0,1},{1,0},{2,3},{3,2},{4,5},{5,4},{6,7},{7,6},{8,9},{9,8},{10,11... | collective-permute-start | bytes 3145736 | tf_op jit(solution)/shard_map/ppermute | solution.py:18
  97.5 17.4 %collective-permute-start.6 = (bf16[1024,256]{1,0:T(8,128)(2,1)S(1)}, bf16[1024,256]{1,0:T(8,128)(2,1)S(1)}, u32[]{:S(2)}, u32[]{:S(2)}) collective-permute-start(bf16[1024,256]{1,0:T(8,128)(2,1)S(1)} %fusion.80), channel_id=1, source_target_pairs={{0,2},{1,3},{8,10},{9,11},{16,18},{17,19},{24,26},{25,27}} | collective-permute-start | bytes 1572872 | tf_op jit(solution)/shard_map/ppermute | solution.py:130
  101.0 13.9 %collective-permute-start.9 = (bf16[1024,256]{1,0:T(8,128)(2,1)S(1)}, bf16[1024,256]{1,0:T(8,128)(2,1)S(1)}, u32[]{:S(2)}, u32[]{:S(2)}) collective-permute-start(bf16[1024,256]{1,0:T(8,128)(2,1)S(1)} %fusion.80), channel_id=1, source_target_pairs={{6,4},{7,5},{14,12},{15,13},{22,20},{23,21},{30,28},{31,29}} | collective-permute-start | bytes 1572872 | tf_op jit(solution)/shard_map/ppermute | solution.py:131
  114.7 17.6 %collective-permute-start.4 = (bf16[2,1024,256]{2,1,0:T(8,128)(2,1)S(1)}, bf16[2,1024,256]{2,1,0:T(8,128)(2,1)S(1)}, u32[]{:S(2)}, u32[]{:S(2)}) collective-permute-start(bf16[2,1024,256]{2,1,0:T(8,128)(2,1)S(1)} %bitcast.167), channel_id=1, source_target_pairs={{0,1},{1,0},{2,3},{3,2},{4,5},{5,4},{6,7},{7,6},{8,9},{9,8},{10,11... | collective-permute-start | bytes 3145736 | tf_op jit(solution)/shard_map/ppermute | solution.py:18
  115.6 16.9 %collective-permute-start.10 = (bf16[1024,256]{1,0:T(8,128)(2,1)S(1)}, bf16[1024,256]{1,0:T(8,128)(2,1)S(1)}, u32[]{:S(2)}, u32[]{:S(2)}) collective-permute-start(bf16[1024,256]{1,0:T(8,128)(2,1)S(1)} %get-tuple-element.52), channel_id=1, source_target_pairs={{4,2},{5,3},{6,4},{7,5},{12,10},{13,11},{14,12},{15,13},{20,18},{2... | collective-permute-start | bytes 1572872 | tf_op jit(solution)/shard_map/ppermute | solution.py:131
  116.3 16.2 %collective-permute-start.7 = (bf16[1024,256]{1,0:T(8,128)(2,1)S(1)}, bf16[1024,256]{1,0:T(8,128)(2,1)S(1)}, u32[]{:S(2)}, u32[]{:S(2)}) collective-permute-start(bf16[1024,256]{1,0:T(8,128)(2,1)S(1)} %get-tuple-element.51), channel_id=1, source_target_pairs={{0,2},{1,3},{2,4},{3,5},{8,10},{9,11},{10,12},{11,13},{16,18},{17,... | collective-permute-start | bytes 1572872 | tf_op jit(solution)/shard_map/ppermute | solution.py:130
  134.2 16.5 %collective-permute-start.11 = (bf16[1024,256]{1,0:T(8,128)(2,1)}, bf16[1024,256]{1,0:T(8,128)(2,1)}, u32[]{:S(2)}, u32[]{:S(2)}) collective-permute-start(bf16[1024,256]{1,0:T(8,128)(2,1)} %get-tuple-element.48), channel_id=1, source_target_pairs={{2,0},{3,1},{4,2},{5,3},{6,4},{7,5},{10,8},{11,9},{12,10},{13,11},... | collective-permute-start | bytes 1572872 | tf_op jit(solution)/shard_map/ppermute | solution.py:131
  135.5 16.4 %collective-permute-start.8 = (bf16[1024,256]{1,0:T(8,128)(2,1)}, bf16[1024,256]{1,0:T(8,128)(2,1)}, u32[]{:S(2)}, u32[]{:S(2)}) collective-permute-start(bf16[1024,256]{1,0:T(8,128)(2,1)} %get-tuple-element.47), channel_id=1, source_target_pairs={{0,2},{1,3},{2,4},{3,5},{4,6},{5,7},{8,10},{9,11},{10,12},{11,13},... | collective-permute-start | bytes 1572872 | tf_op jit(solution)/shard_map/ppermute | solution.py:130
  157.0 33.5 %all-to-all-start = ((bf16[32,64,256]{2,1,0:T(8,128)(2,1)}), bf16[32,64,256]{2,1,0:T(8,128)(2,1)}, u32[]{:S(2)}, u32[]{:S(2)}) async-start(bf16[32,64,256]{2,1,0:T(8,128)(2,1)} %bitcast.178), calls=%async_computation | async-start | bytes 2097152 | tf_op jit(solution)/shard_map/all_to_all | solution.py:282
  163.1 2.9 collective-permute-start.15
  163.3 41.6 %collective-permute-start.14 = (bf16[2,1024,256]{2,1,0:T(8,128)(2,1)}, bf16[2,1024,256]{2,1,0:T(8,128)(2,1)}, u32[]{:S(2)}, u32[]{:S(2)}) collective-permute-start(bf16[2,1024,256]{2,1,0:T(8,128)(2,1)} %bitcast.165), channel_id=1, source_target_pairs={{0,1},{1,0},{2,3},{3,2},{4,5},{5,4},{6,7},{7,6},{8,9},{9,8},{10,11... | collective-permute-start | bytes 3145736 | tf_op jit(solution)/shard_map/ppermute | solution.py:18
  165.9 24.6 %copy-start.24 = (s32[2048]{0:T(1024)S(1)}, s32[2048]{0:T(1024)}, u32[]{:S(2)}) copy-start(s32[2048]{0:T(1024)} %select_n.358) | copy-start | bytes 24580
  170.2 29.4 %collective-permute-start.16 = (bf16[1024,256]{1,0:T(8,128)(2,1)}, bf16[1024,256]{1,0:T(8,128)(2,1)S(1)}, u32[]{:S(2)}, u32[]{:S(2)}) collective-permute-start(bf16[1024,256]{1,0:T(8,128)(2,1)} %fusion.81), channel_id=1, source_target_pairs={{0,2},{1,3},{8,10},{9,11},{16,18},{17,19},{24,26},{25,27}} | collective-permute-start | bytes 1572872 | tf_op jit(solution)/shard_map/ppermute | solution.py:130
  173.8 25.7 %collective-permute-start.19 = (bf16[1024,256]{1,0:T(8,128)(2,1)}, bf16[1024,256]{1,0:T(8,128)(2,1)S(1)}, u32[]{:S(2)}, u32[]{:S(2)}) collective-permute-start(bf16[1024,256]{1,0:T(8,128)(2,1)} %fusion.81), channel_id=1, source_target_pairs={{6,4},{7,5},{14,12},{15,13},{22,20},{23,21},{30,28},{31,29}} | collective-permute-start | bytes 1572872 | tf_op jit(solution)/shard_map/ppermute | solution.py:131
  199.5 25.3 %collective-permute-start.12 = (bf16[2,2,2,2,128,256]{5,4,3,2,0,1:T(8,128)(2,1)}, bf16[2,2,2,2,128,256]{5,4,3,2,0,1:T(8,128)(2,1)}, u32[]{:S(2)}, u32[]{:S(2)}) collective-permute-start(bf16[2,2,2,2,128,256]{5,4,3,2,0,1:T(8,128)(2,1)} %fusion.61), channel_id=1, source_target_pairs={{0,1},{1,0},{2,3},{3,2},{4,5},{5,4},{6,7},{7,6},{8,9},{9,8},{10,11... | collective-permute-start | bytes 3145736 | tf_op jit(solution)/shard_map/ppermute | solution.py:18
  202.9 13.0 %collective-permute-start.17 = (bf16[1024,256]{1,0:T(8,128)(2,1)}, bf16[1024,256]{1,0:T(8,128)(2,1)S(1)}, u32[]{:S(2)}, u32[]{:S(2)}) collective-permute-start(bf16[1024,256]{1,0:T(8,128)(2,1)} %get-tuple-element.49), channel_id=1, source_target_pairs={{0,2},{1,3},{2,4},{3,5},{8,10},{9,11},{10,12},{11,13},{16,18},{17,... | collective-permute-start | bytes 1572872 | tf_op jit(solution)/shard_map/ppermute | solution.py:130
  204.2 11.6 %collective-permute-start.20 = (bf16[1024,256]{1,0:T(8,128)(2,1)}, bf16[1024,256]{1,0:T(8,128)(2,1)S(1)}, u32[]{:S(2)}, u32[]{:S(2)}) collective-permute-start(bf16[1024,256]{1,0:T(8,128)(2,1)} %get-tuple-element.50), channel_id=1, source_target_pairs={{4,2},{5,3},{6,4},{7,5},{12,10},{13,11},{14,12},{15,13},{20,18},{2... | collective-permute-start | bytes 1572872 | tf_op jit(solution)/shard_map/ppermute | solution.py:131
  216.3 16.9 %collective-permute-start.18 = (bf16[1024,256]{1,0:T(8,128)(2,1)S(1)}, bf16[1024,256]{1,0:T(8,128)(2,1)}, u32[]{:S(2)}, u32[]{:S(2)}) collective-permute-start(bf16[1024,256]{1,0:T(8,128)(2,1)S(1)} %get-tuple-element.45), channel_id=1, source_target_pairs={{0,2},{1,3},{2,4},{3,5},{4,6},{5,7},{8,10},{9,11},{10,12},{11,13},... | collective-permute-start | bytes 1572872 | tf_op jit(solution)/shard_map/ppermute | solution.py:130
  223.4 14.9 %collective-permute-start.21 = (bf16[1024,256]{1,0:T(8,128)(2,1)S(1)}, bf16[1024,256]{1,0:T(8,128)(2,1)}, u32[]{:S(2)}, u32[]{:S(2)}) collective-permute-start(bf16[1024,256]{1,0:T(8,128)(2,1)S(1)} %get-tuple-element.46), channel_id=1, source_target_pairs={{2,0},{3,1},{4,2},{5,3},{6,4},{7,5},{10,8},{11,9},{12,10},{13,11},... | collective-permute-start | bytes 1572872 | tf_op jit(solution)/shard_map/ppermute | solution.py:131
  228.6 13.1 %collective-permute-start.13 = (bf16[2,2,2,128,256]{4,3,2,1,0:T(8,128)(2,1)}, bf16[2,2,2,128,256]{4,3,2,1,0:T(8,128)(2,1)}, u32[]{:S(2)}, u32[]{:S(2)}) collective-permute-start(bf16[2,2,2,128,256]{4,3,2,1,0:T(8,128)(2,1)} %fusion.77), channel_id=1, source_target_pairs={{0,8},{8,0},{16,24},{24,16},{1,9},{9,1},{17,25},{25,17},{2,10},{10... | collective-permute-start | bytes 1572872 | tf_op jit(solution)/shard_map/ppermute | solution.py:18
  288.9 2.9 collective-permute-start.25
  294.9 15.1 %collective-permute-start.26 = (bf16[2,2,2,128,256]{4,3,2,1,0:T(8,128)(2,1)}, bf16[2,2,2,128,256]{4,3,2,1,0:T(8,128)(2,1)}, u32[]{:S(2)}, u32[]{:S(2)}) collective-permute-start(bf16[2,2,2,128,256]{4,3,2,1,0:T(8,128)(2,1)} %fusion.78), channel_id=1, source_target_pairs={{0,16},{8,24},{16,0},{24,8},{1,17},{9,25},{17,1},{25,9},{2,18},{10... | collective-permute-start | bytes 1572872 | tf_op jit(solution)/shard_map/ppermute | solution.py:18
  295.5 19.2 %collective-permute-start.22 = (bf16[2,2,128,256]{3,2,1,0:T(8,128)(2,1)S(1)}, bf16[2,2,128,256]{3,2,1,0:T(8,128)(2,1)S(1)}, u32[]{:S(2)}, u32[]{:S(2)}) collective-permute-start(bf16[2,2,128,256]{3,2,1,0:T(8,128)(2,1)S(1)} %fusion.85), channel_id=1, source_target_pairs={{0,16},{8,24},{16,0},{24,8},{1,17},{9,25},{17,1},{25,9},{2,18},{10... | collective-permute-start | bytes 786440 | tf_op jit(solution)/shard_map/ppermute | solution.py:18
  311.2 6.7 %collective-permute-start.27 = (bf16[2,2,128,256]{3,2,1,0:T(8,128)(2,1)S(1)}, bf16[2,2,128,256]{3,2,1,0:T(8,128)(2,1)S(1)}, u32[]{:S(2)}, u32[]{:S(2)}) collective-permute-start(bf16[2,2,128,256]{3,2,1,0:T(8,128)(2,1)S(1)} %fusion.86), channel_id=1, source_target_pairs={{0,8},{8,0},{16,24},{24,16},{1,9},{9,1},{17,25},{25,17},{2,10},{10... | collective-permute-start | bytes 786440 | tf_op jit(solution)/shard_map/ppermute | solution.py:18
  314.7 18.1 %collective-permute-start.23 = (f32[2,128,256]{2,1,0:T(8,128)S(1)}, f32[2,128,256]{2,1,0:T(8,128)S(1)}, u32[]{:S(2)}, u32[]{:S(2)}) collective-permute-start(f32[2,128,256]{2,1,0:T(8,128)S(1)} %dynamic-slice_bitcast_fusion.1), channel_id=1, source_target_pairs={{0,4},{1,5},{2,6},{3,7},{4,0},{5,1},{6,2},{7,3},{8,12},{9,13},{10,... | collective-permute-start | bytes 786440 | tf_op jit(solution)/shard_map/ppermute | solution.py:18
  318.0 20.5 %collective-permute-start.28 = (f32[2,128,256]{2,1,0:T(8,128)S(1)}, f32[2,128,256]{2,1,0:T(8,128)S(1)}, u32[]{:S(2)}, u32[]{:S(2)}) collective-permute-start(f32[2,128,256]{2,1,0:T(8,128)S(1)} %dynamic-slice_bitcast_fusion), channel_id=1, source_target_pairs={{0,4},{1,5},{2,6},{3,7},{4,0},{5,1},{6,2},{7,3},{8,12},{9,13},{10,... | collective-permute-start | bytes 786440 | tf_op jit(solution)/shard_map/ppermute | solution.py:18
  333.0 8.3 %collective-permute-start.24 = (f32[128,256]{1,0:T(8,128)S(1)}, f32[128,256]{1,0:T(8,128)S(1)}, u32[]{:S(2)}, u32[]{:S(2)}) collective-permute-start(f32[128,256]{1,0:T(8,128)S(1)} %dynamic-slice_bitcast_fusion.3), channel_id=1, source_target_pairs={{0,2},{1,3},{2,0},{3,1},{4,6},{5,7},{6,4},{7,5},{8,10},{9,11},{10,... | collective-permute-start | bytes 393224 | tf_op jit(solution)/shard_map/ppermute | solution.py:18
  338.6 5.5 %collective-permute-start.29 = (f32[128,256]{1,0:T(8,128)S(1)}, f32[128,256]{1,0:T(8,128)S(1)}, u32[]{:S(2)}, u32[]{:S(2)}) collective-permute-start(f32[128,256]{1,0:T(8,128)S(1)} %dynamic-slice_bitcast_fusion.2), channel_id=1, source_target_pairs={{0,2},{1,3},{2,0},{3,1},{4,6},{5,7},{6,4},{7,5},{8,10},{9,11},{10,... | collective-permute-start | bytes 393224 | tf_op jit(solution)/shard_map/ppermute | solution.py:18
  (25 other events, 174.2 us)
